TPU v7x, 512 devices: a whole 4x8x8 slice. The times are simulated.
512 devices in a mesh: pb: 16 (over y, x_lo), item: 32 (over x_hi, z, core).
Axes of the slice: x: 4 (x_hi: 2, x_lo: 2; x = x_hi * 2 + x_lo), y: 8, z: 8, core: 2. Of those that a mesh axis runs over, the one named last changes fastest.
Arguments:
- queries: bfloat16 [8192, 512], P(('pb', 'item')), may hold values from -2 to 2
- gate_query: bfloat16 [8192, 64], P(('pb', 'item')), may hold values from -6 to 250
- items: bfloat16 [16384, 512], P(('item', 'pb')), may hold values from -2 to 2
- gate_items: bfloat16 [16384, 64], P(('item', 'pb')), may hold values from -6 to 6
- slot_tiles: int32 [16, 192], P('pb', 'item'), may hold values from -1 to 15, as said below
- d_scores: bfloat16 [16, 192, 128, 128], P('pb', 'item'), may hold values from -6 to 6
Outputs:
- grad_queries: bfloat16 [8192, 512], P(('pb', 'item'))
- grad_gate_query: float32 [8192, 64], P(('pb', 'item'))
- grad_items: bfloat16 [16384, 512], P(('item', 'pb'))
- grad_gate_items: float32 [16384, 64], P(('item', 'pb'))
Inputs may be any that keep to these rules, and one draw needn't show every extreme that they name: `slot_tiles`: each device's row of slots names distinct tiles, live ones first and -1 after them. Devices (p, j) and (p, j + 32 / 2) form a pair: either one of them has all 6 slots live and the other exactly one, or both have between 1 and 3 live slots. Device (0, 0) has all 6 live.
All inputs are finite; a program needn't handle non-finite values.
Results may differ from a plain program's by a relative error of at most 0.0049.
Values may be sent and summed in bfloat16 or wider, within the bound.
No kernel may reach another device: no remote copies, remote signals or barrier semaphores. Data moves between devices by JAX's collectives and lax.ppermute only.
A program may use at most 64 MiB of HBM per device.

v0:
```python
import jax
import jax.numpy as jnp
from jax import lax
from jax.sharding import PartitionSpec as P

E = 64
KQ = 8
KI = 8


def tile_grads(query_tile, query_gate, item_tile, item_gate, cotangent):
    extent = query_tile.shape[0]
    query_parts = query_tile.reshape(extent, KQ, E)
    item_parts = item_tile.reshape(extent, KI, E)
    logits = jnp.einsum(
        "qae,ibe->abqi", query_parts, item_parts, preferred_element_type=jnp.float32
    ).reshape(KQ * KI, extent, extent)
    gates = (
        query_gate.astype(jnp.float32).T[:, :, None] + item_gate.astype(jnp.float32).T[:, None, :]
    )
    weights = jax.nn.softmax(gates, axis=0)
    score = jnp.sum(weights * logits, axis=0)
    upstream = cotangent.astype(jnp.float32)[None]
    logit_grad = (upstream * weights).astype(jnp.bfloat16)
    gate_grad = upstream * weights * (logits - score[None])
    logit_parts = logit_grad.reshape(KQ, KI, extent, extent)
    query_grad = jnp.einsum(
        "abqi,ibe->qae", logit_parts, item_parts, preferred_element_type=jnp.float32
    ).reshape(extent, KQ * E)
    item_grad = jnp.einsum(
        "abqi,qae->ibe", logit_parts, query_parts, preferred_element_type=jnp.float32
    ).reshape(extent, KI * E)
    return (query_grad, jnp.sum(gate_grad, axis=2).T, item_grad, jnp.sum(gate_grad, axis=1).T)


def on_device(queries, gate_query, items, gate_items, slot_tiles, d_scores):
    block_queries, block_gates = (
        lax.all_gather(queries, "item", axis=0, tiled=True),
        lax.all_gather(gate_query, "item", axis=0, tiled=True),
    )
    shard_items, shard_gates = (
        lax.all_gather(items, "pb", axis=0, tiled=True),
        lax.all_gather(gate_items, "pb", axis=0, tiled=True),
    )
    extent = d_scores.shape[-1]
    tile_ids = slot_tiles.reshape(-1)
    cotangents = d_scores.reshape(-1, extent, extent)
    slot_count = tile_ids.shape[0]
    item_blocks = shard_items.shape[0] // extent

    def anchors(tile_id):
        safe_id = jnp.maximum(tile_id, 0)
        return (safe_id // item_blocks * extent, safe_id % item_blocks * extent)

    def operands(tile_id):
        query_start, item_start = anchors(tile_id)
        return (
            lax.dynamic_slice_in_dim(block_queries, query_start, extent, 0),
            lax.dynamic_slice_in_dim(block_gates, query_start, extent, 0),
            lax.dynamic_slice_in_dim(shard_items, item_start, extent, 0),
            lax.dynamic_slice_in_dim(shard_gates, item_start, extent, 0),
        )

    def accumulate(current, tile_id, grads):
        query_start, item_start = anchors(tile_id)
        starts = (query_start, query_start, item_start, item_start)
        return tuple(
            (
                lax.dynamic_update_slice_in_dim(
                    total, lax.dynamic_slice_in_dim(total, start, extent, 0) + update, start, 0
                )
                for total, update, start in zip(current, grads, starts)
            )
        )

    totals = (
        jnp.zeros(block_queries.shape, jnp.float32),
        jnp.zeros(block_gates.shape, jnp.float32),
        jnp.zeros(shard_items.shape, jnp.float32),
        jnp.zeros(shard_gates.shape, jnp.float32),
    )

    def home_step(position, current):
        tile_id = tile_ids[position]

        def work(state):
            return accumulate(state, tile_id, tile_grads(*operands(tile_id), cotangents[position]))

        return lax.cond(tile_id >= 0, work, lambda state: state, current)

    totals = lax.fori_loop(0, slot_count, home_step, totals)
    query_sum, query_gate_sum = (
        lax.psum_scatter(totals[0], "item", scatter_dimension=0, tiled=True),
        lax.psum_scatter(totals[1], "item", scatter_dimension=0, tiled=True),
    )
    item_sum, item_gate_sum = (
        lax.psum_scatter(totals[2], "pb", scatter_dimension=0, tiled=True),
        lax.psum_scatter(totals[3], "pb", scatter_dimension=0, tiled=True),
    )
    return (
        query_sum.astype(jnp.bfloat16),
        query_gate_sum,
        item_sum.astype(jnp.bfloat16),
        item_gate_sum,
    )


def solution(mesh):
    return jax.shard_map(
        on_device,
        mesh=mesh,
        in_specs=(
            P(("pb", "item"), None),
            P(("pb", "item"), None),
            P(("item", "pb"), None),
            P(("item", "pb"), None),
            P("pb", "item"),
            P("pb", "item", None, None),
        ),
        out_specs=(
            P(("pb", "item"), None),
            P(("pb", "item"), None),
            P(("item", "pb"), None),
            P(("item", "pb"), None),
        ),
        check_vma=False,
    )
```

profile of v0, /device:TPU:1, one launch (start us, length us, event | category | flops | bytes accessed | tf_op | source)
XLA Modules:
  0.0 654.5 jit_solution(1207350731947987089)
XLA Ops:
  7.2 49.8 %all_gather.13 = bf16[512,64]{1,0:T(8,128)(2,1)S(1)} all-gather(bf16[16,64]{1,0:T(8,128)(2,1)} %param.11), channel_id=1, replica_groups=mesh['pb'=16,'item'=32] {'item'}, dimensions={0}, use_global_device_ids=true | all-gather | bytes 67584 | tf_op jit(solution)/shard_map/all_gather | solution.py:39
  57.1 26.7 %all_gather.14 = bf16[512,64]{1,0:T(8,128)(2,1)S(1)} all-gather(bf16[32,64]{1,0:T(8,128)(2,1)} %param.13), channel_id=1, replica_groups=mesh['pb'=16,'item'=32] {'pb'}, dimensions={0}, use_global_device_ids=true | all-gather | bytes 69632 | tf_op jit(solution)/shard_map/all_gather | solution.py:43
  84.6 1.7 copy.60
  86.3 45.3 %all_gather.15 = bf16[512,512]{1,0:T(8,128)(2,1)S(1)} all-gather(bf16[16,512]{1,0:T(8,128)(2,1)} %param.10), channel_id=1, replica_groups=mesh['pb'=16,'item'=32] {'item'}, dimensions={0}, use_global_device_ids=true | all-gather | bytes 540672 | tf_op jit(solution)/shard_map/all_gather | solution.py:38
  131.8 26.4 %all_gather.12 = bf16[512,512]{1,0:T(8,128)(2,1)S(1)} all-gather(bf16[32,512]{1,0:T(8,128)(2,1)} %param.12), channel_id=1, replica_groups=mesh['pb'=16,'item'=32] {'pb'}, dimensions={0}, use_global_device_ids=true | all-gather | bytes 557056 | tf_op jit(solution)/shard_map/all_gather | solution.py:42
  159.9 22.5 %while.19 = (s32[]{:T(128)}, f32[512,512]{0,1:T(8,128)S(1)}, f32[512,64]{0,1:T(8,128)}, f32[512,512]{0,1:T(8,128)S(1)}, f32[512,64]{0,1:T(8,128)}, /*index=5*/s3...) while((s32[]{:T(128)}, f32[512,512]{0,1:T(8,128)S(1)}, ...), condition=%wide.region_8.9_spmd, body=%wide.region_0.8_spmd.sunk | while | flops 432128032 | bytes 13894240 | solution.py:91
  161.2 14.8 %conditional.2 = ((f32[512,512]{0,1:T(8,128)S(1)}, f32[512,64]{0,1:T(8,128)}, f32[512,512]{0,1:T(8,128)S(1)}, f32[512,64]{0,1:T(8,128)})) conditional(s32[]{:T(128)} %convert_element_type.27, (f32[512,512]{0,1:T(8,128)S(1)}, f32[512,64]{0,1:T(8,128)}, f32[512,512]{0,1:T(8,128)S(1)}, f32[512,64]{0,1:T(8,128)}) %tuple.50, (s32[]{:T(128)}, ...), branch_computations={%region_1.0_spmd, %region_2.7_spmd} | conditional | flops 432128032 | bytes 13893961 | solution.py:89
  164.7 1.3 fusion.1
  166.2 1.3 fusion.7
  167.5 1.3 fusion.6
  169.0 1.3 fusion.2
  170.3 2.9 fusion.4
  173.3 1.4 fusion.8
  174.7 1.4 fusion.9
  182.4 1.3 copy.65
  183.8 1.4 copy.67
  185.3 1.8 copy.66
  187.1 1.7 copy.68
  188.9 189.1 %reduce-scatter.5.cloned.1.call-done = f32[16,512]{1,0:T(8,128)} async-done(((f32[512,512]{1,0:T(8,128)}), f32[16,512]{1,0:T(8,128)}) %reduce-scatter.5.cloned.1.call-update) | async-done | bytes 32784 | tf_op jit(solution)/shard_map/reduce_scatter | solution.py:93
  377.9 1.4 convert_element_type.21
  379.3 68.0 %reduce-scatter.9.cloned.1.call-done = f32[32,512]{1,0:T(8,128)} async-done(((f32[512,512]{1,0:T(8,128)}), f32[32,512]{1,0:T(8,128)}) %reduce-scatter.9.cloned.1.call-update) | async-done | bytes 65552 | tf_op jit(solution)/shard_map/reduce_scatter | solution.py:97
  447.3 1.5 convert_element_type.22
  448.8 132.1 %reduce-scatter.7.cloned.1.call-done = f32[16,64]{1,0:T(8,128)} async-done(((f32[512,64]{1,0:T(8,128)}), f32[16,64]{1,0:T(8,128)}) %reduce-scatter.7.cloned.1.call-update) | async-done | bytes 4112 | tf_op jit(solution)/shard_map/reduce_scatter | solution.py:94
  580.8 67.1 %reduce-scatter.11.cloned.1.call-done = f32[32,64]{1,0:T(8,128)} async-done(((f32[512,64]{1,0:T(8,128)}), f32[32,64]{1,0:T(8,128)}) %reduce-scatter.11.cloned.1.call-update) | async-done | bytes 8208 | tf_op jit(solution)/shard_map/reduce_scatter | solution.py:98
  (39 shorter events, 9.7 us)
Async XLA Ops:
  7.2 152.8 %copy-start = (s32[1,6]{1,0:T(1,128)S(1)}, s32[1,6]{1,0:T(1,128)}, u32[]{:S(2)}) copy-start(s32[1,6]{1,0:T(1,128)} %param.14) | copy-start | bytes 76
  7.2 370.7 %reduce-scatter.5.cloned.1.call-start = ((), (), s32[]{:S(2)}) async-start(), calls=%async_computation.4 | async-start | bytes 1081344 | tf_op jit(solution)/shard_map/reduce_scatter | solution.py:93
  183.8 263.6 %reduce-scatter.9.cloned.1.call-start = ((), (), s32[]{:S(2)}) async-start(), calls=%async_computation.6 | async-start | bytes 1114112 | tf_op jit(solution)/shard_map/reduce_scatter | solution.py:97
  185.2 395.6 %reduce-scatter.7.cloned.1.call-start = ((), (), s32[]{:S(2)}) async-start(), calls=%async_computation.5 | async-start | bytes 270336 | tf_op jit(solution)/shard_map/reduce_scatter | solution.py:94
  187.0 460.9 %reduce-scatter.11.cloned.1.call-start = ((), (), s32[]{:S(2)}) async-start(), calls=%async_computation.7 | async-start | bytes 278528 | tf_op jit(solution)/shard_map/reduce_scatter | solution.py:98
Sparse Core Ops, SparseCore 0:
  183.9 193.9 reduce-scatter.4
  380.7 66.5 reduce-scatter.8
  452.5 128.2 reduce-scatter.6
  584.0 63.8 reduce-scatter.10
where the time goes:
time: 666 us; the launch traced here: 654 us
  waiting for transfers between devices  456 us (68%)
  blocking collectives  148 us (22%)
  local copies, waits for them, and re-layouts  14.5 us (2%)
  between operations  13.8 us (2%)
  other arithmetic  12.6 us (2%)
    reduce_scatter x1, waiting for transfers between devices, on_device(): lax.psum_scatter(totals[0], 'item', scatter_dimension=0, tiled=True)  189 us
    reduce_scatter x1, waiting for transfers between devices, on_device(): lax.psum_scatter(totals[1], 'item', scatter_dimension=0, tiled=True)  132 us
    reduce_scatter x1, waiting for transfers between devices, on_device(): lax.psum_scatter(totals[2], 'pb', scatter_dimension=0, tiled=True)  68 us
    reduce_scatter x1, waiting for transfers between devices, on_device(): lax.psum_scatter(totals[3], 'pb', scatter_dimension=0, tiled=True)  67.1 us
    all_gather x1, blocking collectives, on_device(): lax.all_gather(gate_query, 'item', axis=0, tiled=True)  49.8 us
    all_gather x1, blocking collectives, on_device(): lax.all_gather(queries, 'item', axis=0, tiled=True)  45.3 us
    all_gather x1, blocking collectives, on_device(): lax.all_gather(gate_items, 'pb', axis=0, tiled=True)  26.7 us
    all_gather x1, blocking collectives, on_device(): lax.all_gather(items, 'pb', axis=0, tiled=True)  26.4 us
  transfers between devices with their start and end apart: 4, of which 4 were waited for; matrix products, arithmetic and copies ran while one was open for 1% of the time, Pallas kernels for 0%

commit v1 on v0

--- a/solution.py
+++ b/solution.py
@@ -34,14 +34,23 @@
 
 
 def on_device(queries, gate_query, items, gate_items, slot_tiles, d_scores):
-    block_queries, block_gates = (
-        lax.all_gather(queries, "item", axis=0, tiled=True),
-        lax.all_gather(gate_query, "item", axis=0, tiled=True),
-    )
-    shard_items, shard_gates = (
-        lax.all_gather(items, "pb", axis=0, tiled=True),
-        lax.all_gather(gate_items, "pb", axis=0, tiled=True),
-    )
+    def fetch(rows, gates, axis):
+        width = rows.shape[1]
+        packed = jnp.concatenate([rows, gates], axis=1)
+        copies = jnp.tile(packed, (lax.axis_size(axis), 1))
+        whole = lax.all_to_all(copies, axis, 0, 0, tiled=True)
+        return whole[:, :width], whole[:, width:]
+
+    def give(rows, gates, axis):
+        width = rows.shape[1]
+        packed = jnp.concatenate([rows, gates], axis=1).astype(jnp.bfloat16)
+        terms = lax.all_to_all(packed, axis, 0, 0, tiled=True)
+        terms = terms.reshape(lax.axis_size(axis), -1, packed.shape[1])
+        total = jnp.sum(terms.astype(jnp.float32), axis=0)
+        return total[:, :width].astype(jnp.bfloat16), total[:, width:]
+
+    block_queries, block_gates = fetch(queries, gate_query, "item")
+    shard_items, shard_gates = fetch(items, gate_items, "pb")
     extent = d_scores.shape[-1]
     tile_ids = slot_tiles.reshape(-1)
     cotangents = d_scores.reshape(-1, extent, extent)
@@ -89,20 +98,9 @@
         return lax.cond(tile_id >= 0, work, lambda state: state, current)
 
     totals = lax.fori_loop(0, slot_count, home_step, totals)
-    query_sum, query_gate_sum = (
-        lax.psum_scatter(totals[0], "item", scatter_dimension=0, tiled=True),
-        lax.psum_scatter(totals[1], "item", scatter_dimension=0, tiled=True),
-    )
-    item_sum, item_gate_sum = (
-        lax.psum_scatter(totals[2], "pb", scatter_dimension=0, tiled=True),
-        lax.psum_scatter(totals[3], "pb", scatter_dimension=0, tiled=True),
-    )
-    return (
-        query_sum.astype(jnp.bfloat16),
-        query_gate_sum,
-        item_sum.astype(jnp.bfloat16),
-        item_gate_sum,
-    )
+    query_sum, query_gate_sum = give(totals[0], totals[1], "item")
+    item_sum, item_gate_sum = give(totals[2], totals[3], "pb")
+    return query_sum, query_gate_sum, item_sum, item_gate_sum
 
 
 def solution(mesh):

time: 666 us -> 221 us (0.33); the launches traced: 654 us -> 218 us
  waiting for transfers between devices: 456 us -> 71.3 us
  blocking collectives: 148 us -> 0 us
  other arithmetic: 12.6 us -> 64.3 us
  starting transfers between devices: 0.16 us -> 35.6 us
  matrix products: 3.98 us -> 23.9 us
  between operations: 13.8 us -> 0.79 us
    reduce_scatter x4 -> x0, waiting for transfers between devices: 456 us -> none  [the longest x1 189 us: on_device(): lax.psum_scatter(totals[0], 'item', scatter_dimension=0, tiled=True)]
    all_gather x4 -> x0, blocking collectives: 148 us -> none  [the longest x1 49.8 us: on_device(): lax.all_gather(gate_query, 'item', axis=0, tiled=True)]
    all_to_all x0 -> x4, waiting for transfers between devices: none -> 71.3 us  [the longest x2 36.7 us: fetch(): whole = lax.all_to_all(copies, axis, 0, 0, tiled=True)]
    all_to_all x0 -> x4, starting transfers between devices: none -> 35.6 us  [the longest x2 24.4 us: fetch(): whole = lax.all_to_all(copies, axis, 0, 0, tiled=True)]
    reduce_sum x1 -> x6, other arithmetic: 2.92 us -> 17.5 us  [tile_grads(): jnp.sum(gate_grad, axis=1)]
    dynamic_update_slice x4 -> x24, other arithmetic: 2.89 us -> 17.5 us  [accumulate(): lax.dynamic_update_slice_in_dim(total, lax.dynamic_slice_in_dim(total, st...]
    dot_general x1 -> x6, matrix products: 1.34 us -> 8.09 us  [tile_grads(): jnp.einsum('abqi,qae->ibe', logit_parts, query_parts, preferred_element_t...]
    dot_general x1 -> x6, matrix products: 1.34 us -> 8.03 us  [tile_grads(): jnp.einsum('abqi,ibe->qae', logit_parts, item_parts, preferred_element_ty...]
  transfers between devices with their start and end apart: 4 -> 4, of which waited for: 4 -> 4; matrix products, arithmetic and copies ran while one was open for 1% -> 2% of each run, Pallas kernels for 0% -> 0%
where the time goes in v1:
time: 221 us; the launch traced here: 218 us
  waiting for transfers between devices  71.3 us (32%)
  other arithmetic  64.3 us (29%)
  starting transfers between devices  35.6 us (16%)
  matrix products  23.9 us (11%)
  local copies, waits for them, and re-layouts  13.5 us (6%)
  loops' own time  8.66 us (4%)
    all_to_all x2, waiting for transfers between devices, fetch(): whole = lax.all_to_all(copies, axis, 0, 0, tiled=True)  36.7 us
    all_to_all x2, waiting for transfers between devices, give(): terms = lax.all_to_all(packed, axis, 0, 0, tiled=True)  34.6 us
    all_to_all x2, starting transfers between devices, fetch(): whole = lax.all_to_all(copies, axis, 0, 0, tiled=True)  24.4 us
    reduce_sum x6, other arithmetic, tile_grads(): jnp.sum(gate_grad, axis=1)  17.5 us
    dynamic_update_slice x24, other arithmetic, accumulate(): lax.dynamic_update_slice_in_dim(total, lax.dynamic_slice_in_dim(total, st...  17.5 us
    all_to_all x2, starting transfers between devices, give(): terms = lax.all_to_all(packed, axis, 0, 0, tiled=True)  11.2 us
    dot_general x6, matrix products, tile_grads(): jnp.einsum('abqi,qae->ibe', logit_parts, query_parts, preferred_element_t...  8.09 us
    dot_general x6, matrix products, tile_grads(): jnp.einsum('abqi,ibe->qae', logit_parts, item_parts, preferred_element_ty...  8.03 us
  transfers between devices with their start and end apart: 4, of which 4 were waited for; matrix products, arithmetic and copies ran while one was open for 2% of the time, Pallas kernels for 0%

profile of v1, /device:TPU:1, one launch (start us, length us, event | category | flops | bytes accessed | tf_op | source)
XLA Modules:
  0.0 218.2 jit_solution(15152412975944647266)
XLA Ops:
  2.3 8.7 %all-to-all-start = ((bf16[16,32,576]{2,1,0:T(8,128)(2,1)}), bf16[16,32,576]{2,1,0:T(8,128)(2,1)S(1)}, u32[]{:S(2)}, u32[]{:S(2)}) async-start(bf16[16,32,576]{2,1,0:T(8,128)(2,1)} %tile.4), calls=%async_computation | async-start | bytes 1310720 | tf_op jit(solution)/shard_map/all_to_all | solution.py:41
  11.8 17.5 %all-to-all-done = bf16[16,32,576]{2,1,0:T(8,128)(2,1)S(1)} async-done(((bf16[16,32,576]{2,1,0:T(8,128)(2,1)}), bf16[16,32,576]{2,1,0:T(8,128)(2,1)S(1)}, u32[]{:S(2)}, u32[]{:S(2)}) %all-to-all-start) | async-done | bytes 589856 | tf_op jit(solution)/shard_map/all_to_all | solution.py:41
  30.1 15.7 %all-to-all-start.1 = ((bf16[32,16,576]{2,1,0:T(8,128)(2,1)}), bf16[32,16,576]{2,1,0:T(8,128)(2,1)S(1)}, u32[]{:S(2)}, u32[]{:S(2)}) async-start(bf16[32,16,576]{2,1,0:T(8,128)(2,1)} %tile.5), calls=%async_computation.1 | async-start | bytes 1310720 | tf_op jit(solution)/shard_map/all_to_all | solution.py:41
  47.1 19.2 %all-to-all-done.1 = bf16[32,16,576]{2,1,0:T(8,128)(2,1)S(1)} async-done(((bf16[32,16,576]{2,1,0:T(8,128)(2,1)}), bf16[32,16,576]{2,1,0:T(8,128)(2,1)S(1)}, u32[]{:S(2)}, u32[]{:S(2)}) %all-to-all-start.1) | async-done | bytes 589856 | tf_op jit(solution)/shard_map/all_to_all | solution.py:41
  68.9 96.5 %while.19 = (s32[]{:T(128)}, f32[512,512]{0,1:T(8,128)S(1)}, f32[512,64]{0,1:T(8,128)}, f32[512,512]{0,1:T(8,128)S(1)}, f32[512,64]{0,1:T(8,128)}, /*index=5*/s3...) while((s32[]{:T(128)}, f32[512,512]{0,1:T(8,128)S(1)}, ...), condition=%wide.region_8.9_spmd, body=%wide.region_0.8_spmd.sunk | while | flops 432128032 | bytes 13894240 | solution.py:100
  70.2 14.8 %conditional.2 = ((f32[512,512]{0,1:T(8,128)S(1)}, f32[512,64]{0,1:T(8,128)}, f32[512,512]{0,1:T(8,128)S(1)}, f32[512,64]{0,1:T(8,128)})) conditional(s32[]{:T(128)} %convert_element_type.35, (f32[512,512]{0,1:T(8,128)S(1)}, f32[512,64]{0,1:T(8,128)}, f32[512,512]{0,1:T(8,128)S(1)}, f32[512,64]{0,1:T(8,128)}) %tuple.53, (s32[]{:T(128)}, ...), branch_computations={%region_1.0_spmd, %region_2.7_spmd} | conditional | flops 432128032 | bytes 13893961 | solution.py:98
  79.3 2.9 %fusion.4 = (f32[8,8,128]{2,0,1:T(8,128)S(1)}, f32[8,8,128]{2,0,1:T(8,128)S(1)}) fusion(f32[128,128]{0,1:T(8,128)S(1)} %get-tuple-element.331, f32[128,8,128,8]{2,0,3,1:T(8,128)S(1)} %get-tuple-element.332, f32[128,128]{0,1:T(8,128)S(1)} %copy.69, f32[128,128]{0,1:T(8,128)S(1)} %copy.68, f32[8,8,128]{2,0,1:T(8,128)S(1)} %copy.67, f32[8,8,128]{2,0,1:T(8,128)S(1)} %copy.66, ...), kind=kLoop, calls=%fused_computation.10 | loop fusion | flops 8372224 | bytes 4587520 | tf_op jit(solution)/shard_map/while/body/eval_jaxpr/cond/branch_1_fun/reduce_sum | solution.py:33
  82.2 1.4 fusion.8
  86.2 14.8 %conditional.2 = ((f32[512,512]{0,1:T(8,128)S(1)}, f32[512,64]{0,1:T(8,128)}, f32[512,512]{0,1:T(8,128)S(1)}, f32[512,64]{0,1:T(8,128)})) conditional(s32[]{:T(128)} %convert_element_type.35, (f32[512,512]{0,1:T(8,128)S(1)}, f32[512,64]{0,1:T(8,128)}, f32[512,512]{0,1:T(8,128)S(1)}, f32[512,64]{0,1:T(8,128)}) %tuple.53, (s32[]{:T(128)}, ...), branch_computations={%region_1.0_spmd, %region_2.7_spmd} | conditional | flops 432128032 | bytes 13893961 | solution.py:98
  95.4 2.9 %fusion.4 = (f32[8,8,128]{2,0,1:T(8,128)S(1)}, f32[8,8,128]{2,0,1:T(8,128)S(1)}) fusion(f32[128,128]{0,1:T(8,128)S(1)} %get-tuple-element.331, f32[128,8,128,8]{2,0,3,1:T(8,128)S(1)} %get-tuple-element.332, f32[128,128]{0,1:T(8,128)S(1)} %copy.69, f32[128,128]{0,1:T(8,128)S(1)} %copy.68, f32[8,8,128]{2,0,1:T(8,128)S(1)} %copy.67, f32[8,8,128]{2,0,1:T(8,128)S(1)} %copy.66, ...), kind=kLoop, calls=%fused_computation.10 | loop fusion | flops 8372224 | bytes 4587520 | tf_op jit(solution)/shard_map/while/body/eval_jaxpr/cond/branch_1_fun/reduce_sum | solution.py:33
  98.3 1.4 fusion.8
  102.3 14.8 %conditional.2 = ((f32[512,512]{0,1:T(8,128)S(1)}, f32[512,64]{0,1:T(8,128)}, f32[512,512]{0,1:T(8,128)S(1)}, f32[512,64]{0,1:T(8,128)})) conditional(s32[]{:T(128)} %convert_element_type.35, (f32[512,512]{0,1:T(8,128)S(1)}, f32[512,64]{0,1:T(8,128)}, f32[512,512]{0,1:T(8,128)S(1)}, f32[512,64]{0,1:T(8,128)}) %tuple.53, (s32[]{:T(128)}, ...), branch_computations={%region_1.0_spmd, %region_2.7_spmd} | conditional | flops 432128032 | bytes 13893961 | solution.py:98
  111.4 2.9 %fusion.4 = (f32[8,8,128]{2,0,1:T(8,128)S(1)}, f32[8,8,128]{2,0,1:T(8,128)S(1)}) fusion(f32[128,128]{0,1:T(8,128)S(1)} %get-tuple-element.331, f32[128,8,128,8]{2,0,3,1:T(8,128)S(1)} %get-tuple-element.332, f32[128,128]{0,1:T(8,128)S(1)} %copy.69, f32[128,128]{0,1:T(8,128)S(1)} %copy.68, f32[8,8,128]{2,0,1:T(8,128)S(1)} %copy.67, f32[8,8,128]{2,0,1:T(8,128)S(1)} %copy.66, ...), kind=kLoop, calls=%fused_computation.10 | loop fusion | flops 8372224 | bytes 4587520 | tf_op jit(solution)/shard_map/while/body/eval_jaxpr/cond/branch_1_fun/reduce_sum | solution.py:33
  114.4 1.4 fusion.8
  118.4 14.8 %conditional.2 = ((f32[512,512]{0,1:T(8,128)S(1)}, f32[512,64]{0,1:T(8,128)}, f32[512,512]{0,1:T(8,128)S(1)}, f32[512,64]{0,1:T(8,128)})) conditional(s32[]{:T(128)} %convert_element_type.35, (f32[512,512]{0,1:T(8,128)S(1)}, f32[512,64]{0,1:T(8,128)}, f32[512,512]{0,1:T(8,128)S(1)}, f32[512,64]{0,1:T(8,128)}) %tuple.53, (s32[]{:T(128)}, ...), branch_computations={%region_1.0_spmd, %region_2.7_spmd} | conditional | flops 432128032 | bytes 13893961 | solution.py:98
  127.5 2.9 %fusion.4 = (f32[8,8,128]{2,0,1:T(8,128)S(1)}, f32[8,8,128]{2,0,1:T(8,128)S(1)}) fusion(f32[128,128]{0,1:T(8,128)S(1)} %get-tuple-element.331, f32[128,8,128,8]{2,0,3,1:T(8,128)S(1)} %get-tuple-element.332, f32[128,128]{0,1:T(8,128)S(1)} %copy.69, f32[128,128]{0,1:T(8,128)S(1)} %copy.68, f32[8,8,128]{2,0,1:T(8,128)S(1)} %copy.67, f32[8,8,128]{2,0,1:T(8,128)S(1)} %copy.66, ...), kind=kLoop, calls=%fused_computation.10 | loop fusion | flops 8372224 | bytes 4587520 | tf_op jit(solution)/shard_map/while/body/eval_jaxpr/cond/branch_1_fun/reduce_sum | solution.py:33
  134.5 14.8 %conditional.2 = ((f32[512,512]{0,1:T(8,128)S(1)}, f32[512,64]{0,1:T(8,128)}, f32[512,512]{0,1:T(8,128)S(1)}, f32[512,64]{0,1:T(8,128)})) conditional(s32[]{:T(128)} %convert_element_type.35, (f32[512,512]{0,1:T(8,128)S(1)}, f32[512,64]{0,1:T(8,128)}, f32[512,512]{0,1:T(8,128)S(1)}, f32[512,64]{0,1:T(8,128)}) %tuple.53, (s32[]{:T(128)}, ...), branch_computations={%region_1.0_spmd, %region_2.7_spmd} | conditional | flops 432128032 | bytes 13893961 | solution.py:98
  143.6 2.9 %fusion.4 = (f32[8,8,128]{2,0,1:T(8,128)S(1)}, f32[8,8,128]{2,0,1:T(8,128)S(1)}) fusion(f32[128,128]{0,1:T(8,128)S(1)} %get-tuple-element.331, f32[128,8,128,8]{2,0,3,1:T(8,128)S(1)} %get-tuple-element.332, f32[128,128]{0,1:T(8,128)S(1)} %copy.69, f32[128,128]{0,1:T(8,128)S(1)} %copy.68, f32[8,8,128]{2,0,1:T(8,128)S(1)} %copy.67, f32[8,8,128]{2,0,1:T(8,128)S(1)} %copy.66, ...), kind=kLoop, calls=%fused_computation.10 | loop fusion | flops 8372224 | bytes 4587520 | tf_op jit(solution)/shard_map/while/body/eval_jaxpr/cond/branch_1_fun/reduce_sum | solution.py:33
  150.5 14.8 %conditional.2 = ((f32[512,512]{0,1:T(8,128)S(1)}, f32[512,64]{0,1:T(8,128)}, f32[512,512]{0,1:T(8,128)S(1)}, f32[512,64]{0,1:T(8,128)})) conditional(s32[]{:T(128)} %convert_element_type.35, (f32[512,512]{0,1:T(8,128)S(1)}, f32[512,64]{0,1:T(8,128)}, f32[512,512]{0,1:T(8,128)S(1)}, f32[512,64]{0,1:T(8,128)}) %tuple.53, (s32[]{:T(128)}, ...), branch_computations={%region_1.0_spmd, %region_2.7_spmd} | conditional | flops 432128032 | bytes 13893961 | solution.py:98
  159.7 2.9 %fusion.4 = (f32[8,8,128]{2,0,1:T(8,128)S(1)}, f32[8,8,128]{2,0,1:T(8,128)S(1)}) fusion(f32[128,128]{0,1:T(8,128)S(1)} %get-tuple-element.331, f32[128,8,128,8]{2,0,3,1:T(8,128)S(1)} %get-tuple-element.332, f32[128,128]{0,1:T(8,128)S(1)} %copy.69, f32[128,128]{0,1:T(8,128)S(1)} %copy.68, f32[8,8,128]{2,0,1:T(8,128)S(1)} %copy.67, f32[8,8,128]{2,0,1:T(8,128)S(1)} %copy.66, ...), kind=kLoop, calls=%fused_computation.10 | loop fusion | flops 8372224 | bytes 4587520 | tf_op jit(solution)/shard_map/while/body/eval_jaxpr/cond/branch_1_fun/reduce_sum | solution.py:33
  167.5 3.6 %all-to-all-start.3 = ((bf16[16,32,576]{2,1,0:T(8,128)(2,1)}), bf16[16,32,576]{2,1,0:T(8,128)(2,1)S(1)}, u32[]{:S(2)}, u32[]{:S(2)}) async-start(bf16[16,32,576]{2,1,0:T(8,128)(2,1)} %pad_maximum_fusion.1), calls=%async_computation.3 | async-start | bytes 1310720 | tf_op jit(solution)/shard_map/all_to_all | solution.py:47
  173.3 15.3 %all-to-all-done.3 = bf16[16,32,576]{2,1,0:T(8,128)(2,1)S(1)} async-done(((bf16[16,32,576]{2,1,0:T(8,128)(2,1)}), bf16[16,32,576]{2,1,0:T(8,128)(2,1)S(1)}, u32[]{:S(2)}, u32[]{:S(2)}) %all-to-all-start.3) | async-done | bytes 589856 | tf_op jit(solution)/shard_map/all_to_all | solution.py:47
  188.6 7.6 %all-to-all-start.2 = ((bf16[32,16,576]{2,1,0:T(8,128)(2,1)}), bf16[32,16,576]{2,1,0:T(8,128)(2,1)S(1)}, u32[]{:S(2)}, u32[]{:S(2)}) async-start(bf16[32,16,576]{2,1,0:T(8,128)(2,1)} %pad_maximum_fusion), calls=%async_computation.2 | async-start | bytes 1310720 | tf_op jit(solution)/shard_map/all_to_all | solution.py:47
  197.6 19.3 %all-to-all-done.2 = bf16[32,16,576]{2,1,0:T(8,128)(2,1)S(1)} async-done(((bf16[32,16,576]{2,1,0:T(8,128)(2,1)}), bf16[32,16,576]{2,1,0:T(8,128)(2,1)S(1)}, u32[]{:S(2)}, u32[]{:S(2)}) %all-to-all-start.2) | async-done | bytes 589856 | tf_op jit(solution)/shard_map/all_to_all | solution.py:47
  (134 shorter events, 80.1 us)
Async XLA Ops:
  0.6 45.3 %copy-start = (bf16[1,6,128,128]{3,2,1,0:T(8,128)(2,1)S(1)}, bf16[1,6,128,128]{3,2,1,0:T(8,128)(2,1)}, u32[]{:S(2)}) copy-start(bf16[1,6,128,128]{3,2,1,0:T(8,128)(2,1)} %param.15) | copy-start | bytes 589828
  2.3 26.9 %all-to-all-start = ((bf16[16,32,576]{2,1,0:T(8,128)(2,1)}), bf16[16,32,576]{2,1,0:T(8,128)(2,1)S(1)}, u32[]{:S(2)}, u32[]{:S(2)}) async-start(bf16[16,32,576]{2,1,0:T(8,128)(2,1)} %tile.4), calls=%async_computation | async-start | bytes 1310720 | tf_op jit(solution)/shard_map/all_to_all | solution.py:41
  30.1 36.2 %all-to-all-start.1 = ((bf16[32,16,576]{2,1,0:T(8,128)(2,1)}), bf16[32,16,576]{2,1,0:T(8,128)(2,1)S(1)}, u32[]{:S(2)}, u32[]{:S(2)}) async-start(bf16[32,16,576]{2,1,0:T(8,128)(2,1)} %tile.5), calls=%async_computation.1 | async-start | bytes 1310720 | tf_op jit(solution)/shard_map/all_to_all | solution.py:41
  45.9 23.0 %copy-start.1 = (s32[1,6]{1,0:T(1,128)S(1)}, s32[1,6]{1,0:T(1,128)}, u32[]{:S(2)}) copy-start(s32[1,6]{1,0:T(1,128)} %param.14) | copy-start | bytes 76
  167.5 21.1 %all-to-all-start.3 = ((bf16[16,32,576]{2,1,0:T(8,128)(2,1)}), bf16[16,32,576]{2,1,0:T(8,128)(2,1)S(1)}, u32[]{:S(2)}, u32[]{:S(2)}) async-start(bf16[16,32,576]{2,1,0:T(8,128)(2,1)} %pad_maximum_fusion.1), calls=%async_computation.3 | async-start | bytes 1310720 | tf_op jit(solution)/shard_map/all_to_all | solution.py:47
  188.6 28.2 %all-to-all-start.2 = ((bf16[32,16,576]{2,1,0:T(8,128)(2,1)}), bf16[32,16,576]{2,1,0:T(8,128)(2,1)S(1)}, u32[]{:S(2)}, u32[]{:S(2)}) async-start(bf16[32,16,576]{2,1,0:T(8,128)(2,1)} %pad_maximum_fusion), calls=%async_computation.2 | async-start | bytes 1310720 | tf_op jit(solution)/shard_map/all_to_all | solution.py:47

commit v2 on v1

v2 whole, which is shorter than its diff:
```python
import jax
import jax.numpy as jnp
from jax import lax
from jax.experimental import pallas as pl
from jax.experimental.pallas import tpu as pltpu
from jax.sharding import PartitionSpec as P

E = 64
KQ = 8
KI = 8
F32 = jnp.float32
BF = jnp.bfloat16
LANES_OF_BOTH = (((1,), (1,)), ((), ()))


def split(x):
    high = x.astype(BF)
    return high, (x - high.astype(F32)).astype(BF)


def dot(a, b):
    return jnp.dot(a, b, preferred_element_type=F32)


def dot_lanes(a, b):
    return lax.dot_general(a, b, LANES_OF_BOTH, preferred_element_type=F32)


def tile_kernel(
    ids, q_ref, i_ref, t_ref, gq_ref, gi_ref,
    qt, it, eqt, eit, vt, xt, tile_t, n_q, n_i, n_0, ft, fit, acc_q, acc_i, weight,
):
    rows = q_ref.shape[0]
    cols = i_ref.shape[0]
    extent = t_ref.shape[-1]
    width = KQ * E
    comps = KQ * KI
    blocks = cols // extent
    step = 2 * E
    chunk = KI * step

    tile_t[...] = jnp.zeros_like(tile_t)
    for slot in range(t_ref.shape[0]):
        tile_id = ids[slot]

        @pl.when(tile_id >= 0)
        def _():
            tile_t[tile_id] = t_ref[slot].astype(F32)

    gates = q_ref[:, width:].astype(F32)
    eq = jnp.exp(gates - jnp.max(gates, axis=1, keepdims=True))
    gates_t = gates.T
    eqt[...] = jnp.exp(gates_t - jnp.max(gates_t, axis=0, keepdims=True))
    eit[...] = jnp.exp(i_ref[:, width:].astype(F32).T)
    qt[...] = q_ref[:, :width].astype(F32).T
    it[...] = i_ref[:, :width].astype(F32).T

    eq_hi, eq_mid = split(eq)
    eq_lo = (eq - eq_hi.astype(F32) - eq_mid.astype(F32)).astype(BF)
    ei_hi, ei_lo = split(eit[...])
    eqt_hi, eqt_lo = split(eqt[...])
    norm = dot(
        jnp.concatenate([eq_hi, eq_hi, eq_mid], axis=1),
        jnp.concatenate([ei_hi, ei_lo, ei_hi], axis=0),
    )
    parts = jnp.concatenate([eq_hi, eq_mid, eq_lo], axis=1)
    part_row = lax.broadcasted_iota(jnp.int32, (3 * comps, chunk), 0) % comps
    part_lane = lax.broadcasted_iota(jnp.int32, (3 * comps, chunk), 1)
    lane_comp = (part_lane // E) % 2 * KI + part_lane // step

    n_0[...] = jnp.zeros_like(n_0)
    n_q[...] = jnp.zeros_like(n_q)
    n_i[...] = jnp.zeros_like(n_i)

    def spread(ap, carry):
        pick = jnp.where(part_row == lane_comp + 2 * KI * ap, 1.0, 0.0).astype(BF)
        scale = dot(parts, pick)
        own = q_ref[:, pl.ds(pl.multiple_of(ap * step, step), step)].astype(F32)
        x_hi, x_lo = split(scale * jnp.concatenate([own] * KI, axis=1))
        lows = []
        highs = []
        for b in range(KI):
            for half in range(2):
                comp = (2 * ap + half) * KI + b
                v = it[b * E:(b + 1) * E, :] * eit[pl.ds(comp, 1), :]
                v_hi, v_lo = split(v)
                highs.append(v_hi)
                lows.append(v_lo)
                at = pl.multiple_of(ap * chunk + b * step + half * E, E)
                a_at = pl.multiple_of((2 * ap + half) * E, E)
                x = qt[pl.ds(a_at, E), :] * eqt[pl.ds(comp, 1), :]
                xt[pl.ds(at, E), :] = x.astype(BF)
        v_hi = jnp.concatenate(highs, axis=0)
        v_lo = jnp.concatenate(lows, axis=0)
        vt[pl.ds(pl.multiple_of(ap * chunk, chunk), chunk), :] = v_hi
        n_0[...] += dot(x_hi, v_hi)
        n_q[...] += dot(x_lo, v_hi)
        n_i[...] += dot(x_hi, v_lo)
        return carry

    lax.fori_loop(0, KQ // 2, spread, 0)

    lines = []
    for r in range(rows // extent):
        lines.append(
            jnp.concatenate([tile_t[r * blocks + c] for c in range(blocks)], axis=1)
        )
    inverse = 1.0 / norm
    weight[...] = (jnp.concatenate(lines, axis=0) * inverse).astype(BF)
    rounded = weight[...].astype(F32) * inverse
    whole = n_0[...]
    wq_hi, wq_lo = split(rounded * (whole + n_q[...]))
    wi_hi, wi_lo = split(rounded * (whole + n_i[...]))
    mean_q = dot_lanes(ei_hi, wq_hi) + dot_lanes(ei_lo, wq_hi) + dot_lanes(ei_hi, wq_lo)
    mean_i = dot(eqt_hi, wi_hi) + dot(eqt_lo, wi_hi) + dot(eqt_hi, wi_lo)

    acc_i[...] = jnp.zeros_like(acc_i)

    def collect(ap, carry):
        at = pl.ds(pl.multiple_of(ap * chunk, chunk), chunk)
        u = dot_lanes(vt[at, :], weight[...])
        w = dot(xt[at, :], weight[...])
        for half in range(2):
            a = 2 * ap + half
            a_rows = pl.ds(pl.multiple_of(a * E, E), E)
            own = qt[a_rows, :]
            total = jnp.zeros((E, rows), F32)
            sums_q = []
            sums_i = []
            for b in range(KI):
                low = b * step + half * E
                comp = a * KI + b
                u_part = u[low:low + E, :]
                w_part = w[low:low + E, :]
                total += u_part * eqt[pl.ds(comp, 1), :]
                acc_i[b * E:(b + 1) * E, :] += w_part * eit[pl.ds(comp, 1), :]
                sums_q.append(jnp.sum(u_part * own, axis=0, keepdims=True))
                sums_i.append(jnp.sum(w_part * it[b * E:(b + 1) * E, :], axis=0, keepdims=True))
            acc_q[a_rows, :] = total
            comp_rows = pl.ds(pl.multiple_of(a * KI, KI), KI)
            ft[comp_rows, :] = jnp.concatenate(sums_q, axis=0)
            fit[comp_rows, :] = jnp.concatenate(sums_i, axis=0)
        return carry

    lax.fori_loop(0, KQ // 2, collect, 0)

    gq_ref[:, :width] = acc_q[...].T.astype(BF)
    gi_ref[:, :width] = acc_i[...].T.astype(BF)
    gq_ref[:, width:] = (eqt[...] * (ft[...] - mean_q)).T.astype(BF)
    gi_ref[:, width:] = (eit[...] * (fit[...] - mean_i)).T.astype(BF)


def tile_grads(tile_ids, cotangents, block, shard, interpret=False):
    rows, packed = block.shape
    cols = shard.shape[0]
    width = KQ * E
    comps = KQ * KI
    extent = cotangents.shape[-1]
    vmem = pl.BlockSpec(memory_space=pltpu.VMEM)
    return pl.pallas_call(
        tile_kernel,
        out_shape=(
            jax.ShapeDtypeStruct((rows, packed), BF),
            jax.ShapeDtypeStruct((cols, packed), BF),
        ),
        in_specs=[pl.BlockSpec(memory_space=pltpu.SMEM), vmem, vmem, vmem],
        out_specs=(vmem, vmem),
        scratch_shapes=[
            pltpu.VMEM((width, rows), F32),
            pltpu.VMEM((width, cols), F32),
            pltpu.VMEM((comps, rows), F32),
            pltpu.VMEM((comps, cols), F32),
            pltpu.VMEM((comps * E, cols), BF),
            pltpu.VMEM((comps * E, rows), BF),
            pltpu.VMEM((rows * cols // extent**2, extent, extent), F32),
            pltpu.VMEM((rows, cols), F32),
            pltpu.VMEM((rows, cols), F32),
            pltpu.VMEM((rows, cols), F32),
            pltpu.VMEM((comps, rows), F32),
            pltpu.VMEM((comps, cols), F32),
            pltpu.VMEM((width, rows), F32),
            pltpu.VMEM((width, cols), F32),
            pltpu.VMEM((rows, cols), BF),
        ],
        compiler_params=pltpu.CompilerParams(vmem_limit_bytes=56 * 2**20),
        interpret=interpret,
    )(tile_ids, block, shard, cotangents)


def fetch(rows, gates, axis):
    packed = jnp.concatenate([rows, gates], axis=1)
    copies = jnp.tile(packed, (lax.axis_size(axis), 1))
    return lax.all_to_all(copies, axis, 0, 0, tiled=True)


def give(packed, width, axis):
    terms = lax.all_to_all(packed, axis, 0, 0, tiled=True)
    terms = terms.reshape(lax.axis_size(axis), -1, packed.shape[1])
    total = jnp.sum(terms.astype(F32), axis=0)
    return total[:, :width].astype(BF), total[:, width:]


def on_device(queries, gate_query, items, gate_items, slot_tiles, d_scores):
    width = queries.shape[1]
    extent = d_scores.shape[-1]
    block = fetch(queries, gate_query, "item")
    shard = fetch(items, gate_items, "pb")
    for_block, for_shard = tile_grads(
        slot_tiles.reshape(-1), d_scores.reshape(-1, extent, extent), block, shard
    )
    query_sum, query_gate_sum = give(for_block, width, "item")
    item_sum, item_gate_sum = give(for_shard, width, "pb")
    return query_sum, query_gate_sum, item_sum, item_gate_sum


def solution(mesh):
    return jax.shard_map(
        on_device,
        mesh=mesh,
        in_specs=(
            P(("pb", "item"), None),
            P(("pb", "item"), None),
            P(("item", "pb"), None),
            P(("item", "pb"), None),
            P("pb", "item"),
            P("pb", "item", None, None),
        ),
        out_specs=(
            P(("pb", "item"), None),
            P(("pb", "item"), None),
            P(("item", "pb"), None),
            P(("item", "pb"), None),
        ),
        check_vma=False,
    )
```

time: 221 us -> 137 us (0.62); the launches traced: 218 us -> 137 us
  other arithmetic: 64.3 us -> 1.01 us
  blocking collectives: 0 us -> 57.7 us
  waiting for transfers between devices: 71.3 us -> 37.3 us
  matrix products: 23.9 us -> 0 us
  Pallas kernels: 0 us -> 19.4 us
  starting transfers between devices: 35.6 us -> 17.2 us
  local copies, waits for them, and re-layouts: 13.5 us -> 3.39 us
  loops' own time: 8.66 us -> 0 us
    all_to_all x0 -> x2, blocking collectives: none -> 57.7 us  [the longest x1 36.1 us: fetch(): return lax.all_to_all(copies, axis, 0, 0, tiled=True)]
    reduce_sum x14 -> x2, other arithmetic: 25.3 us -> 0.22 us  [give(): total = jnp.sum(terms.astype(F32), axis=0)]
    dot_general x18 -> x0, matrix products: 23.9 us -> none  [the longest x6 8.09 us: tile_grads(): jnp.einsum('abqi,qae->ibe', logit_parts, query_parts, preferred_element_t...]
    pallas_call x0 -> x1, Pallas kernels: none -> 19.4 us  [tile_grads(): pl.pallas_call(tile_kernel, out_shape=(jax.ShapeDtypeStruct((rows, packed...]
    all_to_all x2 -> x1, waiting for transfers between devices: 36.7 us -> 18.2 us  [fetch(): return lax.all_to_all(copies, axis, 0, 0, tiled=True)]
    dynamic_update_slice x24 -> x0, other arithmetic: 17.5 us -> none  [accumulate(): lax.dynamic_update_slice_in_dim(total, lax.dynamic_slice_in_dim(total, st...]
    all_to_all x2 -> x1, starting transfers between devices: 24.4 us -> 8.8 us  [fetch(): return lax.all_to_all(copies, axis, 0, 0, tiled=True)]
    all_to_all x2 -> x1, waiting for transfers between devices: 34.6 us -> 19.1 us  [give(): terms = lax.all_to_all(packed, axis, 0, 0, tiled=True)]
  transfers between devices with their start and end apart: 4 -> 2, of which waited for: 4 -> 2; matrix products, arithmetic and copies ran while one was open for 2% -> 1% of each run, Pallas kernels for 0% -> 0%
where the time goes in v2:
time: 137 us
  blocking collectives  57.7 us (42%)
  waiting for transfers between devices  37.3 us (27%)
  Pallas kernels  19.4 us (14%)
  starting transfers between devices  17.2 us (13%)
  local copies, waits for them, and re-layouts  3.39 us (2%)
    all_to_all x1, blocking collectives, fetch(): return lax.all_to_all(copies, axis, 0, 0, tiled=True)  36.1 us
    all_to_all x1, blocking collectives, give(): terms = lax.all_to_all(packed, axis, 0, 0, tiled=True)  21.7 us
    pallas_call x1, Pallas kernels, tile_grads(): pl.pallas_call(tile_kernel, out_shape=(jax.ShapeDtypeStruct((rows, packed...  19.4 us
    all_to_all x1, waiting for transfers between devices, give(): terms = lax.all_to_all(packed, axis, 0, 0, tiled=True)  19.1 us
    all_to_all x1, waiting for transfers between devices, fetch(): return lax.all_to_all(copies, axis, 0, 0, tiled=True)  18.2 us
    all_to_all x1, starting transfers between devices, fetch(): return lax.all_to_all(copies, axis, 0, 0, tiled=True)  8.8 us
    all_to_all x1, starting transfers between devices, give(): terms = lax.all_to_all(packed, axis, 0, 0, tiled=True)  8.41 us
  transfers between devices with their start and end apart: 2, of which 2 were waited for; matrix products, arithmetic and copies ran while one was open for 1% of the time, Pallas kernels for 0%

profile of v2, /device:TPU:1, one launch (start us, length us, event | category | flops | bytes accessed | tf_op | source)
XLA Modules:
  0.0 136.7 jit_solution(11304629811569179378)
XLA Ops:
  0.6 0.8 pad_maximum_fusion
  1.4 0.9 tile.5
  2.3 0.0 copy-start.1
  2.3 0.0 copy-start.2
  2.3 8.8 %all-to-all-start.1 = ((bf16[16,32,576]{2,1,0:T(8,128)(2,1)}), bf16[16,32,576]{2,1,0:T(8,128)(2,1)S(1)}, u32[]{:S(2)}, u32[]{:S(2)}) async-start(bf16[16,32,576]{2,1,0:T(8,128)(2,1)} %tile.5), calls=%async_computation.1 | async-start | bytes 1310720 | tf_op jit(solution)/shard_map/all_to_all | solution.py:193
  11.1 0.0 copy-done.1
  11.1 0.0 copy-done.2
  11.2 18.2 %all-to-all-done.1 = bf16[16,32,576]{2,1,0:T(8,128)(2,1)S(1)} async-done(((bf16[16,32,576]{2,1,0:T(8,128)(2,1)}), bf16[16,32,576]{2,1,0:T(8,128)(2,1)S(1)}, u32[]{:S(2)}, u32[]{:S(2)}) %all-to-all-start.1) | async-done | bytes 589856 | tf_op jit(solution)/shard_map/all_to_all | solution.py:193
  29.4 0.0 copy-start
  29.4 0.1 tile.4
  29.4 36.1 %all_to_all.34 = bf16[32,16,576]{2,1,0:T(8,128)(2,1)} all-to-all(bf16[32,16,576]{2,1,0:T(8,128)(2,1)S(1)} %tile.4), channel_id=1, replica_groups=mesh['pb'=16,'item'=32] {'item'}, dimensions={0} | all-to-all | bytes 1179648 | tf_op jit(solution)/shard_map/all_to_all | solution.py:193
  65.5 0.0 copy-done
  65.5 19.4 %shard_map.93 = (bf16[512,576]{1,0:T(8,128)(2,1)}, bf16[512,576]{1,0:T(8,128)(2,1)}) custom-call(s32[6]{0:T(128)} %bitcast.10, bf16[512,576]{1,0:T(8,128)(2,1)} %bitcast.7, bf16[512,576]{1,0:T(8,128)(2,1)} %bitcast.6, bf16[6,128,128]{2,1,0:T(8,128)(2,1)} %bitcast.9), custom_call_target="tpu_custom_call" | custom-call | tf_op jit(solution)/shard_map/pallas_call | solution.py:160
  84.9 21.7 %all_to_all.35 = bf16[16,32,576]{2,1,0:T(8,128)(2,1)S(1)} all-to-all(bf16[16,32,576]{2,1,0:T(8,128)(2,1)} %bitcast.8), channel_id=1, replica_groups=mesh['pb'=16,'item'=32] {'pb'}, dimensions={0} | all-to-all | bytes 1179648 | tf_op jit(solution)/shard_map/all_to_all | solution.py:197
  106.5 8.4 %all-to-all-start.2 = ((bf16[32,16,576]{2,1,0:T(8,128)(2,1)}), bf16[32,16,576]{2,1,0:T(8,128)(2,1)S(1)}, u32[]{:S(2)}, u32[]{:S(2)}) async-start(bf16[32,16,576]{2,1,0:T(8,128)(2,1)} %bitcast.4), calls=%async_computation.2 | async-start | bytes 1310720 | tf_op jit(solution)/shard_map/all_to_all | solution.py:197
  115.0 0.1 convert_reduce_fusion
  115.1 0.6 slice.21
  115.7 0.6 slice.24
  116.3 19.1 %all-to-all-done.2 = bf16[32,16,576]{2,1,0:T(8,128)(2,1)S(1)} async-done(((bf16[32,16,576]{2,1,0:T(8,128)(2,1)}), bf16[32,16,576]{2,1,0:T(8,128)(2,1)S(1)}, u32[]{:S(2)}, u32[]{:S(2)}) %all-to-all-start.2) | async-done | bytes 589856 | tf_op jit(solution)/shard_map/all_to_all | solution.py:197
  135.4 0.1 convert_reduce_fusion.1
  135.5 0.6 slice.19
  136.1 0.6 slice.25
  (1 shorter events, 0.0 us)
Async XLA Ops:
  2.3 8.8 %copy-start.1 = (bf16[16,512]{1,0:T(8,128)(2,1)S(1)}, bf16[16,512]{1,0:T(8,128)(2,1)}, u32[]{:S(2)}) copy-start(bf16[16,512]{1,0:T(8,128)(2,1)} %param.6) | copy-start | bytes 49156
  2.3 8.8 %copy-start.2 = (bf16[16,64]{1,0:T(8,128)(2,1)S(1)}, bf16[16,64]{1,0:T(8,128)(2,1)}, u32[]{:S(2)}) copy-start(bf16[16,64]{1,0:T(8,128)(2,1)} %param.7) | copy-start | bytes 6148
  2.3 27.0 %all-to-all-start.1 = ((bf16[16,32,576]{2,1,0:T(8,128)(2,1)}), bf16[16,32,576]{2,1,0:T(8,128)(2,1)S(1)}, u32[]{:S(2)}, u32[]{:S(2)}) async-start(bf16[16,32,576]{2,1,0:T(8,128)(2,1)} %tile.5), calls=%async_computation.1 | async-start | bytes 1310720 | tf_op jit(solution)/shard_map/all_to_all | solution.py:193
  29.4 36.1 %copy-start = (bf16[16,32,576]{2,1,0:T(8,128)(2,1)}, bf16[16,32,576]{2,1,0:T(8,128)(2,1)S(1)}, u32[]{:S(2)}) copy-start(bf16[16,32,576]{2,1,0:T(8,128)(2,1)S(1)} %all-to-all-done.1) | copy-start | bytes 1769476
  106.5 28.9 %all-to-all-start.2 = ((bf16[32,16,576]{2,1,0:T(8,128)(2,1)}), bf16[32,16,576]{2,1,0:T(8,128)(2,1)S(1)}, u32[]{:S(2)}, u32[]{:S(2)}) async-start(bf16[32,16,576]{2,1,0:T(8,128)(2,1)} %bitcast.4), calls=%async_computation.2 | async-start | bytes 1310720 | tf_op jit(solution)/shard_map/all_to_all | solution.py:197

commit v3 on v2

--- a/solution.py
+++ b/solution.py
@@ -3,7 +3,9 @@
 from jax import lax
 from jax.experimental import pallas as pl
 from jax.experimental.pallas import tpu as pltpu
+from jax.sharding import Mesh
 from jax.sharding import PartitionSpec as P
+
 
 E = 64
 KQ = 8
@@ -27,9 +29,27 @@
 
 
 def tile_kernel(
-    ids, q_ref, i_ref, t_ref, gq_ref, gi_ref,
+    ids, q_own, q_other, i_own, i_other, t_ref, q_keep, q_send, i_keep, i_send,
+    q_ref, i_ref, gq_ref, gi_ref,
     qt, it, eqt, eit, vt, xt, tile_t, n_q, n_i, n_0, ft, fit, acc_q, acc_i, weight,
 ):
+    core = ids[t_ref.shape[0]]
+    side = ids[t_ref.shape[0] + 1]
+
+    def places(index, whole, half):
+        size = half.shape[1]
+        for g in range(half.shape[0]):
+            mine = pl.multiple_of(g * 2 * size + index * size, size)
+            theirs = pl.multiple_of(g * 2 * size + (1 - index) * size, size)
+            yield g, whole.at[pl.ds(mine, size), :], whole.at[pl.ds(theirs, size), :]
+
+    for g, mine, theirs in places(core, q_ref, q_own):
+        mine[...] = q_own[g]
+        theirs[...] = q_other[g]
+    for g, mine, theirs in places(side, i_ref, i_own):
+        mine[...] = i_own[g]
+        theirs[...] = i_other[g]
+
     rows = q_ref.shape[0]
     cols = i_ref.shape[0]
     extent = t_ref.shape[-1]
@@ -144,15 +164,22 @@
 
     lax.fori_loop(0, KQ // 2, collect, 0)
 
-    gq_ref[:, :width] = acc_q[...].T.astype(BF)
-    gi_ref[:, :width] = acc_i[...].T.astype(BF)
-    gq_ref[:, width:] = (eqt[...] * (ft[...] - mean_q)).T.astype(BF)
-    gi_ref[:, width:] = (eit[...] * (fit[...] - mean_i)).T.astype(BF)
-
-
-def tile_grads(tile_ids, cotangents, block, shard, interpret=False):
-    rows, packed = block.shape
-    cols = shard.shape[0]
+    gq_ref[:, :width] = acc_q[...].T
+    gq_ref[:, width:] = (eqt[...] * (ft[...] - mean_q)).T
+    for g, mine, theirs in places(core, gq_ref, q_keep):
+        q_keep[g] = mine[...]
+        q_send[g] = theirs[...].astype(BF)
+    gi_ref[:, :width] = acc_i[...].T
+    gi_ref[:, width:] = (eit[...] * (fit[...] - mean_i)).T
+    for g, mine, theirs in places(side, gi_ref, i_keep):
+        i_keep[g] = mine[...]
+        i_send[g] = theirs[...].astype(BF)
+
+
+def tile_grads(scalars, cotangents, q_own, q_other, i_own, i_other, interpret=False):
+    packed = q_own.shape[-1]
+    rows = 2 * q_own.shape[0] * q_own.shape[1]
+    cols = 2 * i_own.shape[0] * i_own.shape[1]
     width = KQ * E
     comps = KQ * KI
     extent = cotangents.shape[-1]
@@ -160,12 +187,18 @@
     return pl.pallas_call(
         tile_kernel,
         out_shape=(
-            jax.ShapeDtypeStruct((rows, packed), BF),
-            jax.ShapeDtypeStruct((cols, packed), BF),
+            jax.ShapeDtypeStruct(q_own.shape, F32),
+            jax.ShapeDtypeStruct(q_own.shape, BF),
+            jax.ShapeDtypeStruct(i_own.shape, F32),
+            jax.ShapeDtypeStruct(i_own.shape, BF),
         ),
-        in_specs=[pl.BlockSpec(memory_space=pltpu.SMEM), vmem, vmem, vmem],
-        out_specs=(vmem, vmem),
+        in_specs=[pl.BlockSpec(memory_space=pltpu.SMEM)] + [vmem] * 5,
+        out_specs=(vmem,) * 4,
         scratch_shapes=[
+            pltpu.VMEM((rows, packed), BF),
+            pltpu.VMEM((cols, packed), BF),
+            pltpu.VMEM((rows, packed), F32),
+            pltpu.VMEM((cols, packed), F32),
             pltpu.VMEM((width, rows), F32),
             pltpu.VMEM((width, cols), F32),
             pltpu.VMEM((comps, rows), F32),
@@ -182,20 +215,27 @@
             pltpu.VMEM((width, cols), F32),
             pltpu.VMEM((rows, cols), BF),
         ],
-        compiler_params=pltpu.CompilerParams(vmem_limit_bytes=56 * 2**20),
+        compiler_params=pltpu.CompilerParams(vmem_limit_bytes=40 * 2**20),
         interpret=interpret,
-    )(tile_ids, block, shard, cotangents)
-
-
-def fetch(rows, gates, axis):
+    )(scalars, q_own, q_other, i_own, i_other, cotangents)
+
+
+SWAP = [(0, 1), (1, 0)]
+AXES = (("y", 8), ("x_lo", 2), ("x_hi", 2), ("z", 8), ("core", 2))
+PB = ("y", "x_lo")
+ITEM = ("x_hi", "z", "core")
+
+
+def fetch(rows, gates, axes):
     packed = jnp.concatenate([rows, gates], axis=1)
-    copies = jnp.tile(packed, (lax.axis_size(axis), 1))
-    return lax.all_to_all(copies, axis, 0, 0, tiled=True)
-
-
-def give(packed, width, axis):
-    terms = lax.all_to_all(packed, axis, 0, 0, tiled=True)
-    terms = terms.reshape(lax.axis_size(axis), -1, packed.shape[1])
+    copies = jnp.broadcast_to(packed[None], (lax.axis_size(axes),) + packed.shape)
+    return lax.all_to_all(copies, axes, 0, 0)
+
+
+def give(keep, send, pair, axes, width):
+    got = lax.ppermute(send, pair, SWAP)
+    total = (keep + got.astype(F32)).astype(BF)
+    terms = lax.all_to_all(total, axes, 0, 0)
     total = jnp.sum(terms.astype(F32), axis=0)
     return total[:, :width].astype(BF), total[:, width:]
 
@@ -203,33 +243,31 @@
 def on_device(queries, gate_query, items, gate_items, slot_tiles, d_scores):
     width = queries.shape[1]
     extent = d_scores.shape[-1]
-    block = fetch(queries, gate_query, "item")
-    shard = fetch(items, gate_items, "pb")
-    for_block, for_shard = tile_grads(
-        slot_tiles.reshape(-1), d_scores.reshape(-1, extent, extent), block, shard
-    )
-    query_sum, query_gate_sum = give(for_block, width, "item")
-    item_sum, item_gate_sum = give(for_shard, width, "pb")
+    i_own = fetch(items, gate_items, ("y",))
+    i_other = lax.ppermute(i_own, "x_lo", SWAP)
+    q_own = fetch(queries, gate_query, ("x_hi", "z"))
+    q_other = lax.ppermute(q_own, "core", SWAP)
+    place = [lax.axis_index("core")[None], lax.axis_index("x_lo")[None]]
+    scalars = jnp.concatenate([slot_tiles.reshape(-1)] + place)
+    cotangents = d_scores.reshape(-1, extent, extent)
+    q_keep, q_send, i_keep, i_send = tile_grads(
+        scalars, cotangents, q_own, q_other, i_own, i_other
+    )
+    query_sum, query_gate_sum = give(q_keep, q_send, "core", ("x_hi", "z"), width)
+    item_sum, item_gate_sum = give(i_keep, i_send, "x_lo", ("y",), width)
     return query_sum, query_gate_sum, item_sum, item_gate_sum
 
 
 def solution(mesh):
+    fine = Mesh(
+        mesh.devices.reshape([size for name, size in AXES]), [name for name, size in AXES]
+    )
+    block = P(PB + ITEM, None)
+    shard = P(ITEM + PB, None)
     return jax.shard_map(
         on_device,
-        mesh=mesh,
-        in_specs=(
-            P(("pb", "item"), None),
-            P(("pb", "item"), None),
-            P(("item", "pb"), None),
-            P(("item", "pb"), None),
-            P("pb", "item"),
-            P("pb", "item", None, None),
-        ),
-        out_specs=(
-            P(("pb", "item"), None),
-            P(("pb", "item"), None),
-            P(("item", "pb"), None),
-            P(("item", "pb"), None),
-        ),
+        mesh=fine,
+        in_specs=(block, block, shard, shard, P(PB, ITEM), P(PB, ITEM, None, None)),
+        out_specs=(block, block, shard, shard),
         check_vma=False,
     )

time: 137 us -> 115 us (0.84)
  the two profiles are of different devices: /device:TPU:1 before, /device:TPU:64 now
where the time goes in v3:
time: 115 us
  waiting for transfers between devices  52.3 us (45%)
  starting transfers between devices  36.5 us (32%)
  Pallas kernels  18.1 us (16%)
  local copies, waits for them, and re-layouts  4.6 us (4%)
  other arithmetic  2.57 us (2%)
    all_to_all x2, waiting for transfers between devices, fetch(): return lax.all_to_all(copies, axes, 0, 0)  22.3 us
    all_to_all x2, waiting for transfers between devices, give(): terms = lax.all_to_all(total, axes, 0, 0)  21.9 us
    all_to_all x2, starting transfers between devices, fetch(): return lax.all_to_all(copies, axes, 0, 0)  19.8 us
    pallas_call x1, Pallas kernels, tile_grads(): pl.pallas_call(tile_kernel, out_shape=(jax.ShapeDtypeStruct(q_own.shape,...  18.1 us
    all_to_all x2, starting transfers between devices, give(): terms = lax.all_to_all(total, axes, 0, 0)  7.85 us
    ppermute x2, waiting for transfers between devices, give(): got = lax.ppermute(send, pair, SWAP)  7.21 us
    ppermute x2, starting transfers between devices, give(): got = lax.ppermute(send, pair, SWAP)  4.43 us
    ppermute x1, starting transfers between devices, on_device(): i_other = lax.ppermute(i_own, 'x_lo', SWAP)  2.49 us
  transfers between devices with their start and end apart: 8, of which 6 were waited for; matrix products, arithmetic and copies ran while one was open for 3% of the time, Pallas kernels for 0%

profile of v3, /device:TPU:64, one launch (start us, length us, event | category | flops | bytes accessed | tf_op | source)
XLA Modules:
  0.0 114.7 jit_solution(7911590584552686575)
XLA Ops:
  0.6 0.8 pad_maximum_fusion
  1.4 0.8 broadcast_in_dim.21
  2.2 7.2 %all-to-all-start.1 = ((bf16[8,32,576]{2,1,0:T(8,128)(2,1)}), bf16[8,32,576]{2,1,0:T(8,128)(2,1)S(1)}, u32[]{:S(2)}, u32[]{:S(2)}) async-start(bf16[8,32,576]{2,1,0:T(8,128)(2,1)} %broadcast_in_dim.21), calls=%async_computation.1 | async-start | bytes 655360 | tf_op jit(solution)/shard_map/all_to_all | solution.py:232
  9.4 13.3 %all-to-all-done.1.i_own = bf16[8,32,576]{2,1,0:T(8,128)(2,1)S(1)} async-done(((bf16[8,32,576]{2,1,0:T(8,128)(2,1)}), bf16[8,32,576]{2,1,0:T(8,128)(2,1)S(1)}, u32[]{:S(2)}, u32[]{:S(2)}) %all-to-all-start.1) | async-done | bytes 294944 | tf_op jit(solution)/shard_map/all_to_all | solution.py:232
  22.7 0.8 broadcast_in_dim.20
  23.4 12.6 %all-to-all-start = ((bf16[16,16,576]{2,1,0:T(8,128)(2,1)}), bf16[16,16,576]{2,1,0:T(8,128)(2,1)S(1)}, u32[]{:S(2)}, u32[]{:S(2)}) async-start(bf16[16,16,576]{2,1,0:T(8,128)(2,1)} %broadcast_in_dim.20), calls=%async_computation | async-start | bytes 655360 | tf_op jit(solution)/shard_map/all_to_all | solution.py:232
  36.0 2.5 %collective-permute-start.1 = (bf16[8,32,576]{2,1,0:T(8,128)(2,1)S(1)}, bf16[8,32,576]{2,1,0:T(8,128)(2,1)S(1)}, u32[]{:S(2)}, u32[]{:S(2)}) collective-permute-start(bf16[8,32,576]{2,1,0:T(8,128)(2,1)S(1)} %all-to-all-done.1.i_own), channel_id=1, source_target_pairs={{0,32},{32,0},{1,33},{33,1},{2,34},{34,2},{3,35},{35,3},{4,36},{36... | collective-permute-start | bytes 884744 | tf_op jit(solution)/shard_map/ppermute | solution.py:247
  38.5 9.1 %all-to-all-done.q_own = bf16[16,16,576]{2,1,0:T(8,128)(2,1)S(1)} async-done(((bf16[16,16,576]{2,1,0:T(8,128)(2,1)}), bf16[16,16,576]{2,1,0:T(8,128)(2,1)S(1)}, u32[]{:S(2)}, u32[]{:S(2)}) %all-to-all-start) | async-done | bytes 294944 | tf_op jit(solution)/shard_map/all_to_all | solution.py:232
  47.6 1.9 %collective-permute-start = (bf16[16,16,576]{2,1,0:T(8,128)(2,1)S(1)}, bf16[16,16,576]{2,1,0:T(8,128)(2,1)S(1)}, u32[]{:S(2)}, u32[]{:S(2)}) collective-permute-start(bf16[16,16,576]{2,1,0:T(8,128)(2,1)S(1)} %all-to-all-done.q_own), channel_id=1, source_target_pairs={{0,1},{1,0},{2,3},{3,2},{4,5},{5,4},{6,7},{7,6},{8,9},{9,8},{10,11... | collective-permute-start | bytes 884744 | tf_op jit(solution)/shard_map/ppermute | solution.py:249
  49.5 0.6 copy-done.3
  50.3 0.9 collective-permute-done.q_other
  51.1 18.1 %shard_map.93 = (f32[16,16,576]{2,1,0:T(8,128)S(1)}, bf16[16,16,576]{2,1,0:T(8,128)(2,1)S(1)}, f32[8,32,576]{2,1,0:T(8,128)S(1)}, bf16[8,32,576]{2,1,0:T(8,128)(2,1)S(1)}) custom-call(s32[8]{0:T(128)S(1)} %pad_add_fusion.ids, bf16[16,16,576]{2,1,0:T(8,128)(2,1)S(1)} %all-to-all-done.q_own, bf16[16,16,576]{2,1,0:T(8,128)(2,1)S(1)} %collective-permute-done.q_other, ...), custom_call_target="tpu_custom_call" | custom-call | tf_op jit(solution)/shard_map/pallas_call | solution.py:187
  69.2 2.5 %collective-permute-start.3 = (bf16[8,32,576]{2,1,0:T(8,128)(2,1)S(1)}, bf16[8,32,576]{2,1,0:T(8,128)(2,1)S(1)}, u32[]{:S(2)}, u32[]{:S(2)}) collective-permute-start(bf16[8,32,576]{2,1,0:T(8,128)(2,1)S(1)} %get-tuple-element.11), channel_id=1, source_target_pairs={{0,32},{32,0},{1,33},{33,1},{2,34},{34,2},{3,35},{35,3},{4,36},{36... | collective-permute-start | bytes 884744 | tf_op jit(solution)/shard_map/ppermute | solution.py:236
  71.7 1.9 %collective-permute-start.2 = (bf16[16,16,576]{2,1,0:T(8,128)(2,1)S(1)}, bf16[16,16,576]{2,1,0:T(8,128)(2,1)S(1)}, u32[]{:S(2)}, u32[]{:S(2)}) collective-permute-start(bf16[16,16,576]{2,1,0:T(8,128)(2,1)S(1)} %get-tuple-element.9), channel_id=1, source_target_pairs={{0,1},{1,0},{2,3},{3,2},{4,5},{5,4},{6,7},{7,6},{8,9},{9,8},{10,11... | collective-permute-start | bytes 884744 | tf_op jit(solution)/shard_map/ppermute | solution.py:236
  73.6 7.2 %collective-permute-done.3 = bf16[8,32,576]{2,1,0:T(8,128)(2,1)S(1)} collective-permute-done((bf16[8,32,576]{2,1,0:T(8,128)(2,1)S(1)}, bf16[8,32,576]{2,1,0:T(8,128)(2,1)S(1)}, u32[]{:S(2)}, u32[]{:S(2)}) %collective-permute-start.3) | collective-permute-done | bytes 294944 | tf_op jit(solution)/shard_map/ppermute | solution.py:236
  80.8 0.8 add_convert_fusion
  81.6 3.4 %all-to-all-start.3 = ((bf16[8,32,576]{2,1,0:T(8,128)(2,1)}), bf16[8,32,576]{2,1,0:T(8,128)(2,1)S(1)}, u32[]{:S(2)}, u32[]{:S(2)}) async-start(bf16[8,32,576]{2,1,0:T(8,128)(2,1)} %add_convert_fusion), calls=%async_computation.3 | async-start | bytes 655360 | tf_op jit(solution)/shard_map/all_to_all | solution.py:238
  85.1 0.8 add_convert_fusion.1
  85.9 12.1 %all-to-all-done.3 = bf16[8,32,576]{2,1,0:T(8,128)(2,1)S(1)} async-done(((bf16[8,32,576]{2,1,0:T(8,128)(2,1)}), bf16[8,32,576]{2,1,0:T(8,128)(2,1)S(1)}, u32[]{:S(2)}, u32[]{:S(2)}) %all-to-all-start.3) | async-done | bytes 294944 | tf_op jit(solution)/shard_map/all_to_all | solution.py:238
  98.0 4.4 %all-to-all-start.2 = ((bf16[16,16,576]{2,1,0:T(8,128)(2,1)}), bf16[16,16,576]{2,1,0:T(8,128)(2,1)S(1)}, u32[]{:S(2)}, u32[]{:S(2)}) async-start(bf16[16,16,576]{2,1,0:T(8,128)(2,1)} %add_convert_fusion.1), calls=%async_computation.2 | async-start | bytes 655360 | tf_op jit(solution)/shard_map/all_to_all | solution.py:238
  102.5 0.6 slice.21
  103.1 0.6 slice.24
  103.7 9.7 %all-to-all-done.2 = bf16[16,16,576]{2,1,0:T(8,128)(2,1)S(1)} async-done(((bf16[16,16,576]{2,1,0:T(8,128)(2,1)}), bf16[16,16,576]{2,1,0:T(8,128)(2,1)S(1)}, u32[]{:S(2)}, u32[]{:S(2)}) %all-to-all-start.2) | async-done | bytes 294944 | tf_op jit(solution)/shard_map/all_to_all | solution.py:238
  114.1 0.6 slice.25
  (14 shorter events, 0.8 us)
Async XLA Ops:
  2.2 7.2 %copy-start.1 = (bf16[16,512]{1,0:T(8,128)(2,1)S(1)}, bf16[16,512]{1,0:T(8,128)(2,1)}, u32[]{:S(2)}) copy-start(bf16[16,512]{1,0:T(8,128)(2,1)} %param.6) | copy-start | bytes 49156
  2.2 7.2 %copy-start.2 = (bf16[16,64]{1,0:T(8,128)(2,1)S(1)}, bf16[16,64]{1,0:T(8,128)(2,1)}, u32[]{:S(2)}) copy-start(bf16[16,64]{1,0:T(8,128)(2,1)} %param.7) | copy-start | bytes 6148
  2.2 20.5 %all-to-all-start.1 = ((bf16[8,32,576]{2,1,0:T(8,128)(2,1)}), bf16[8,32,576]{2,1,0:T(8,128)(2,1)S(1)}, u32[]{:S(2)}, u32[]{:S(2)}) async-start(bf16[8,32,576]{2,1,0:T(8,128)(2,1)} %broadcast_in_dim.21), calls=%async_computation.1 | async-start | bytes 655360 | tf_op jit(solution)/shard_map/all_to_all | solution.py:232
  23.4 27.7 %copy-start = (bf16[1,6,128,128]{3,2,1,0:T(8,128)(2,1)S(1)}, bf16[1,6,128,128]{3,2,1,0:T(8,128)(2,1)}, u32[]{:S(2)}) copy-start(bf16[1,6,128,128]{3,2,1,0:T(8,128)(2,1)} %param.11) | copy-start | bytes 589828
  23.4 24.2 %all-to-all-start = ((bf16[16,16,576]{2,1,0:T(8,128)(2,1)}), bf16[16,16,576]{2,1,0:T(8,128)(2,1)S(1)}, u32[]{:S(2)}, u32[]{:S(2)}) async-start(bf16[16,16,576]{2,1,0:T(8,128)(2,1)} %broadcast_in_dim.20), calls=%async_computation | async-start | bytes 655360 | tf_op jit(solution)/shard_map/all_to_all | solution.py:232
  36.0 14.2 %collective-permute-start.1 = (bf16[8,32,576]{2,1,0:T(8,128)(2,1)S(1)}, bf16[8,32,576]{2,1,0:T(8,128)(2,1)S(1)}, u32[]{:S(2)}, u32[]{:S(2)}) collective-permute-start(bf16[8,32,576]{2,1,0:T(8,128)(2,1)S(1)} %all-to-all-done.1.i_own), channel_id=1, source_target_pairs={{0,32},{32,0},{1,33},{33,1},{2,34},{34,2},{3,35},{35,3},{4,36},{36... | collective-permute-start | bytes 884744 | tf_op jit(solution)/shard_map/ppermute | solution.py:247
  47.6 3.5 %collective-permute-start = (bf16[16,16,576]{2,1,0:T(8,128)(2,1)S(1)}, bf16[16,16,576]{2,1,0:T(8,128)(2,1)S(1)}, u32[]{:S(2)}, u32[]{:S(2)}) collective-permute-start(bf16[16,16,576]{2,1,0:T(8,128)(2,1)S(1)} %all-to-all-done.q_own), channel_id=1, source_target_pairs={{0,1},{1,0},{2,3},{3,2},{4,5},{5,4},{6,7},{7,6},{8,9},{9,8},{10,11... | collective-permute-start | bytes 884744 | tf_op jit(solution)/shard_map/ppermute | solution.py:249
  49.5 0.7 copy-start.3
  69.2 11.6 %collective-permute-start.3 = (bf16[8,32,576]{2,1,0:T(8,128)(2,1)S(1)}, bf16[8,32,576]{2,1,0:T(8,128)(2,1)S(1)}, u32[]{:S(2)}, u32[]{:S(2)}) collective-permute-start(bf16[8,32,576]{2,1,0:T(8,128)(2,1)S(1)} %get-tuple-element.11), channel_id=1, source_target_pairs={{0,32},{32,0},{1,33},{33,1},{2,34},{34,2},{3,35},{35,3},{4,36},{36... | collective-permute-start | bytes 884744 | tf_op jit(solution)/shard_map/ppermute | solution.py:236
  71.7 13.4 %collective-permute-start.2 = (bf16[16,16,576]{2,1,0:T(8,128)(2,1)S(1)}, bf16[16,16,576]{2,1,0:T(8,128)(2,1)S(1)}, u32[]{:S(2)}, u32[]{:S(2)}) collective-permute-start(bf16[16,16,576]{2,1,0:T(8,128)(2,1)S(1)} %get-tuple-element.9), channel_id=1, source_target_pairs={{0,1},{1,0},{2,3},{3,2},{4,5},{5,4},{6,7},{7,6},{8,9},{9,8},{10,11... | collective-permute-start | bytes 884744 | tf_op jit(solution)/shard_map/ppermute | solution.py:236
  81.6 16.4 %all-to-all-start.3 = ((bf16[8,32,576]{2,1,0:T(8,128)(2,1)}), bf16[8,32,576]{2,1,0:T(8,128)(2,1)S(1)}, u32[]{:S(2)}, u32[]{:S(2)}) async-start(bf16[8,32,576]{2,1,0:T(8,128)(2,1)} %add_convert_fusion), calls=%async_computation.3 | async-start | bytes 655360 | tf_op jit(solution)/shard_map/all_to_all | solution.py:238
  98.0 15.4 %all-to-all-start.2 = ((bf16[16,16,576]{2,1,0:T(8,128)(2,1)}), bf16[16,16,576]{2,1,0:T(8,128)(2,1)S(1)}, u32[]{:S(2)}, u32[]{:S(2)}) async-start(bf16[16,16,576]{2,1,0:T(8,128)(2,1)} %add_convert_fusion.1), calls=%async_computation.2 | async-start | bytes 655360 | tf_op jit(solution)/shard_map/all_to_all | solution.py:238

commit v4 on v3

--- a/solution.py
+++ b/solution.py
@@ -31,7 +31,7 @@
 def tile_kernel(
     ids, q_own, q_other, i_own, i_other, t_ref, q_keep, q_send, i_keep, i_send,
     q_ref, i_ref, gq_ref, gi_ref,
-    qt, it, eqt, eit, vt, xt, tile_t, n_q, n_i, n_0, ft, fit, acc_q, acc_i, weight,
+    qt, it, eqt, eit, vt, xt, tile_t, n_0, ft, fit, acc_q, acc_i, weight,
 ):
     core = ids[t_ref.shape[0]]
     side = ids[t_ref.shape[0] + 1]
@@ -89,33 +89,22 @@
     lane_comp = (part_lane // E) % 2 * KI + part_lane // step
 
     n_0[...] = jnp.zeros_like(n_0)
-    n_q[...] = jnp.zeros_like(n_q)
-    n_i[...] = jnp.zeros_like(n_i)
 
     def spread(ap, carry):
         pick = jnp.where(part_row == lane_comp + 2 * KI * ap, 1.0, 0.0).astype(BF)
         scale = dot(parts, pick)
         own = q_ref[:, pl.ds(pl.multiple_of(ap * step, step), step)].astype(F32)
-        x_hi, x_lo = split(scale * jnp.concatenate([own] * KI, axis=1))
-        lows = []
-        highs = []
+        x_rows = (scale * jnp.concatenate([own] * KI, axis=1)).astype(BF)
         for b in range(KI):
             for half in range(2):
                 comp = (2 * ap + half) * KI + b
-                v = it[b * E:(b + 1) * E, :] * eit[pl.ds(comp, 1), :]
-                v_hi, v_lo = split(v)
-                highs.append(v_hi)
-                lows.append(v_lo)
                 at = pl.multiple_of(ap * chunk + b * step + half * E, E)
                 a_at = pl.multiple_of((2 * ap + half) * E, E)
                 x = qt[pl.ds(a_at, E), :] * eqt[pl.ds(comp, 1), :]
                 xt[pl.ds(at, E), :] = x.astype(BF)
-        v_hi = jnp.concatenate(highs, axis=0)
-        v_lo = jnp.concatenate(lows, axis=0)
-        vt[pl.ds(pl.multiple_of(ap * chunk, chunk), chunk), :] = v_hi
-        n_0[...] += dot(x_hi, v_hi)
-        n_q[...] += dot(x_lo, v_hi)
-        n_i[...] += dot(x_hi, v_lo)
+                v = it[b * E:(b + 1) * E, :] * eit[pl.ds(comp, 1), :]
+                vt[pl.ds(at, E), :] = v.astype(BF)
+        n_0[...] += dot(x_rows, vt[pl.ds(pl.multiple_of(ap * chunk, chunk), chunk), :])
         return carry
 
     lax.fori_loop(0, KQ // 2, spread, 0)
@@ -127,12 +116,9 @@
         )
     inverse = 1.0 / norm
     weight[...] = (jnp.concatenate(lines, axis=0) * inverse).astype(BF)
-    rounded = weight[...].astype(F32) * inverse
-    whole = n_0[...]
-    wq_hi, wq_lo = split(rounded * (whole + n_q[...]))
-    wi_hi, wi_lo = split(rounded * (whole + n_i[...]))
-    mean_q = dot_lanes(ei_hi, wq_hi) + dot_lanes(ei_lo, wq_hi) + dot_lanes(ei_hi, wq_lo)
-    mean_i = dot(eqt_hi, wi_hi) + dot(eqt_lo, wi_hi) + dot(eqt_hi, wi_lo)
+    w_hi, w_lo = split(weight[...].astype(F32) * inverse * n_0[...])
+    mean_q = dot_lanes(ei_hi, w_hi) + dot_lanes(ei_lo, w_hi) + dot_lanes(ei_hi, w_lo)
+    mean_i = dot(eqt_hi, w_hi) + dot(eqt_lo, w_hi) + dot(eqt_hi, w_lo)
 
     acc_i[...] = jnp.zeros_like(acc_i)
 
@@ -143,7 +129,6 @@
         for half in range(2):
             a = 2 * ap + half
             a_rows = pl.ds(pl.multiple_of(a * E, E), E)
-            own = qt[a_rows, :]
             total = jnp.zeros((E, rows), F32)
             sums_q = []
             sums_i = []
@@ -154,8 +139,11 @@
                 w_part = w[low:low + E, :]
                 total += u_part * eqt[pl.ds(comp, 1), :]
                 acc_i[b * E:(b + 1) * E, :] += w_part * eit[pl.ds(comp, 1), :]
-                sums_q.append(jnp.sum(u_part * own, axis=0, keepdims=True))
-                sums_i.append(jnp.sum(w_part * it[b * E:(b + 1) * E, :], axis=0, keepdims=True))
+                kept = pl.ds(pl.multiple_of(ap * chunk + low, E), E)
+                x = xt[kept, :].astype(F32)
+                v = vt[kept, :].astype(F32)
+                sums_q.append(jnp.sum(u_part * x, axis=0, keepdims=True))
+                sums_i.append(jnp.sum(w_part * v, axis=0, keepdims=True))
             acc_q[a_rows, :] = total
             comp_rows = pl.ds(pl.multiple_of(a * KI, KI), KI)
             ft[comp_rows, :] = jnp.concatenate(sums_q, axis=0)
@@ -165,12 +153,12 @@
     lax.fori_loop(0, KQ // 2, collect, 0)
 
     gq_ref[:, :width] = acc_q[...].T
-    gq_ref[:, width:] = (eqt[...] * (ft[...] - mean_q)).T
+    gq_ref[:, width:] = (ft[...] - eqt[...] * mean_q).T
     for g, mine, theirs in places(core, gq_ref, q_keep):
         q_keep[g] = mine[...]
         q_send[g] = theirs[...].astype(BF)
     gi_ref[:, :width] = acc_i[...].T
-    gi_ref[:, width:] = (eit[...] * (fit[...] - mean_i)).T
+    gi_ref[:, width:] = (fit[...] - eit[...] * mean_i).T
     for g, mine, theirs in places(side, gi_ref, i_keep):
         i_keep[g] = mine[...]
         i_send[g] = theirs[...].astype(BF)
@@ -207,8 +195,6 @@
             pltpu.VMEM((comps * E, rows), BF),
             pltpu.VMEM((rows * cols // extent**2, extent, extent), F32),
             pltpu.VMEM((rows, cols), F32),
-            pltpu.VMEM((rows, cols), F32),
-            pltpu.VMEM((rows, cols), F32),
             pltpu.VMEM((comps, rows), F32),
             pltpu.VMEM((comps, cols), F32),
             pltpu.VMEM((width, rows), F32),

time: 115 us -> 111 us (0.965)
  Pallas kernels: 18.1 us -> 14.1 us
    pallas_call x1, Pallas kernels: 18.1 us -> 14.1 us  [tile_grads(): pl.pallas_call(tile_kernel, out_shape=(jax.ShapeDtypeStruct(q_own.shape,...]
where the time goes in v4:
time: 111 us
  waiting for transfers between devices  52.3 us (47%)
  starting transfers between devices  36.5 us (33%)
  Pallas kernels  14.1 us (13%)
  local copies, waits for them, and re-layouts  4.6 us (4%)
  other arithmetic  2.57 us (2%)
    all_to_all x2, waiting for transfers between devices, fetch(): return lax.all_to_all(copies, axes, 0, 0)  22.3 us
    all_to_all x2, waiting for transfers between devices, give(): terms = lax.all_to_all(total, axes, 0, 0)  21.9 us
    all_to_all x2, starting transfers between devices, fetch(): return lax.all_to_all(copies, axes, 0, 0)  19.8 us
    pallas_call x1, Pallas kernels, tile_grads(): pl.pallas_call(tile_kernel, out_shape=(jax.ShapeDtypeStruct(q_own.shape,...  14.1 us
    all_to_all x2, starting transfers between devices, give(): terms = lax.all_to_all(total, axes, 0, 0)  7.85 us
    ppermute x2, waiting for transfers between devices, give(): got = lax.ppermute(send, pair, SWAP)  7.2 us
    ppermute x2, starting transfers between devices, give(): got = lax.ppermute(send, pair, SWAP)  4.43 us
    ppermute x1, starting transfers between devices, on_device(): i_other = lax.ppermute(i_own, 'x_lo', SWAP)  2.49 us
  transfers between devices with their start and end apart: 8, of which 6 were waited for; matrix products, arithmetic and copies ran while one was open for 3% of the time, Pallas kernels for 0%

profile of v4, /device:TPU:64, one launch (start us, length us, event | category | flops | bytes accessed | tf_op | source)
XLA Modules:
  0.0 110.7 jit_solution(7267885088332275084)
XLA Ops:
  0.6 0.8 pad_maximum_fusion
  1.4 0.8 broadcast_in_dim.21
  2.2 7.2 %all-to-all-start.1 = ((bf16[8,32,576]{2,1,0:T(8,128)(2,1)}), bf16[8,32,576]{2,1,0:T(8,128)(2,1)S(1)}, u32[]{:S(2)}, u32[]{:S(2)}) async-start(bf16[8,32,576]{2,1,0:T(8,128)(2,1)} %broadcast_in_dim.21), calls=%async_computation.1 | async-start | bytes 655360 | tf_op jit(solution)/shard_map/all_to_all | solution.py:218
  9.4 13.3 %all-to-all-done.1.i_own = bf16[8,32,576]{2,1,0:T(8,128)(2,1)S(1)} async-done(((bf16[8,32,576]{2,1,0:T(8,128)(2,1)}), bf16[8,32,576]{2,1,0:T(8,128)(2,1)S(1)}, u32[]{:S(2)}, u32[]{:S(2)}) %all-to-all-start.1) | async-done | bytes 294944 | tf_op jit(solution)/shard_map/all_to_all | solution.py:218
  22.7 0.8 broadcast_in_dim.20
  23.4 12.6 %all-to-all-start = ((bf16[16,16,576]{2,1,0:T(8,128)(2,1)}), bf16[16,16,576]{2,1,0:T(8,128)(2,1)S(1)}, u32[]{:S(2)}, u32[]{:S(2)}) async-start(bf16[16,16,576]{2,1,0:T(8,128)(2,1)} %broadcast_in_dim.20), calls=%async_computation | async-start | bytes 655360 | tf_op jit(solution)/shard_map/all_to_all | solution.py:218
  36.0 2.5 %collective-permute-start.1 = (bf16[8,32,576]{2,1,0:T(8,128)(2,1)S(1)}, bf16[8,32,576]{2,1,0:T(8,128)(2,1)S(1)}, u32[]{:S(2)}, u32[]{:S(2)}) collective-permute-start(bf16[8,32,576]{2,1,0:T(8,128)(2,1)S(1)} %all-to-all-done.1.i_own), channel_id=1, source_target_pairs={{0,32},{32,0},{1,33},{33,1},{2,34},{34,2},{3,35},{35,3},{4,36},{36... | collective-permute-start | bytes 884744 | tf_op jit(solution)/shard_map/ppermute | solution.py:233
  38.5 9.1 %all-to-all-done.q_own = bf16[16,16,576]{2,1,0:T(8,128)(2,1)S(1)} async-done(((bf16[16,16,576]{2,1,0:T(8,128)(2,1)}), bf16[16,16,576]{2,1,0:T(8,128)(2,1)S(1)}, u32[]{:S(2)}, u32[]{:S(2)}) %all-to-all-start) | async-done | bytes 294944 | tf_op jit(solution)/shard_map/all_to_all | solution.py:218
  47.6 1.9 %collective-permute-start = (bf16[16,16,576]{2,1,0:T(8,128)(2,1)S(1)}, bf16[16,16,576]{2,1,0:T(8,128)(2,1)S(1)}, u32[]{:S(2)}, u32[]{:S(2)}) collective-permute-start(bf16[16,16,576]{2,1,0:T(8,128)(2,1)S(1)} %all-to-all-done.q_own), channel_id=1, source_target_pairs={{0,1},{1,0},{2,3},{3,2},{4,5},{5,4},{6,7},{7,6},{8,9},{9,8},{10,11... | collective-permute-start | bytes 884744 | tf_op jit(solution)/shard_map/ppermute | solution.py:235
  49.5 0.6 copy-done.3
  50.3 0.9 collective-permute-done.q_other
  51.1 14.1 %shard_map.93 = (f32[16,16,576]{2,1,0:T(8,128)S(1)}, bf16[16,16,576]{2,1,0:T(8,128)(2,1)S(1)}, f32[8,32,576]{2,1,0:T(8,128)S(1)}, bf16[8,32,576]{2,1,0:T(8,128)(2,1)S(1)}) custom-call(s32[8]{0:T(128)S(1)} %pad_add_fusion.ids, bf16[16,16,576]{2,1,0:T(8,128)(2,1)S(1)} %all-to-all-done.q_own, bf16[16,16,576]{2,1,0:T(8,128)(2,1)S(1)} %collective-permute-done.q_other, ...), custom_call_target="tpu_custom_call" | custom-call | tf_op jit(solution)/shard_map/pallas_call | solution.py:175
  65.2 2.5 %collective-permute-start.3 = (bf16[8,32,576]{2,1,0:T(8,128)(2,1)S(1)}, bf16[8,32,576]{2,1,0:T(8,128)(2,1)S(1)}, u32[]{:S(2)}, u32[]{:S(2)}) collective-permute-start(bf16[8,32,576]{2,1,0:T(8,128)(2,1)S(1)} %get-tuple-element.11), channel_id=1, source_target_pairs={{0,32},{32,0},{1,33},{33,1},{2,34},{34,2},{3,35},{35,3},{4,36},{36... | collective-permute-start | bytes 884744 | tf_op jit(solution)/shard_map/ppermute | solution.py:222
  67.7 1.9 %collective-permute-start.2 = (bf16[16,16,576]{2,1,0:T(8,128)(2,1)S(1)}, bf16[16,16,576]{2,1,0:T(8,128)(2,1)S(1)}, u32[]{:S(2)}, u32[]{:S(2)}) collective-permute-start(bf16[16,16,576]{2,1,0:T(8,128)(2,1)S(1)} %get-tuple-element.9), channel_id=1, source_target_pairs={{0,1},{1,0},{2,3},{3,2},{4,5},{5,4},{6,7},{7,6},{8,9},{9,8},{10,11... | collective-permute-start | bytes 884744 | tf_op jit(solution)/shard_map/ppermute | solution.py:222
  69.6 7.2 %collective-permute-done.3 = bf16[8,32,576]{2,1,0:T(8,128)(2,1)S(1)} collective-permute-done((bf16[8,32,576]{2,1,0:T(8,128)(2,1)S(1)}, bf16[8,32,576]{2,1,0:T(8,128)(2,1)S(1)}, u32[]{:S(2)}, u32[]{:S(2)}) %collective-permute-start.3) | collective-permute-done | bytes 294944 | tf_op jit(solution)/shard_map/ppermute | solution.py:222
  76.8 0.8 add_convert_fusion
  77.6 3.4 %all-to-all-start.3 = ((bf16[8,32,576]{2,1,0:T(8,128)(2,1)}), bf16[8,32,576]{2,1,0:T(8,128)(2,1)S(1)}, u32[]{:S(2)}, u32[]{:S(2)}) async-start(bf16[8,32,576]{2,1,0:T(8,128)(2,1)} %add_convert_fusion), calls=%async_computation.3 | async-start | bytes 655360 | tf_op jit(solution)/shard_map/all_to_all | solution.py:224
  81.1 0.8 add_convert_fusion.1
  81.9 12.1 %all-to-all-done.3 = bf16[8,32,576]{2,1,0:T(8,128)(2,1)S(1)} async-done(((bf16[8,32,576]{2,1,0:T(8,128)(2,1)}), bf16[8,32,576]{2,1,0:T(8,128)(2,1)S(1)}, u32[]{:S(2)}, u32[]{:S(2)}) %all-to-all-start.3) | async-done | bytes 294944 | tf_op jit(solution)/shard_map/all_to_all | solution.py:224
  94.0 4.4 %all-to-all-start.2 = ((bf16[16,16,576]{2,1,0:T(8,128)(2,1)}), bf16[16,16,576]{2,1,0:T(8,128)(2,1)S(1)}, u32[]{:S(2)}, u32[]{:S(2)}) async-start(bf16[16,16,576]{2,1,0:T(8,128)(2,1)} %add_convert_fusion.1), calls=%async_computation.2 | async-start | bytes 655360 | tf_op jit(solution)/shard_map/all_to_all | solution.py:224
  98.5 0.6 slice.21
  99.1 0.6 slice.24
  99.7 9.8 %all-to-all-done.2 = bf16[16,16,576]{2,1,0:T(8,128)(2,1)S(1)} async-done(((bf16[16,16,576]{2,1,0:T(8,128)(2,1)}), bf16[16,16,576]{2,1,0:T(8,128)(2,1)S(1)}, u32[]{:S(2)}, u32[]{:S(2)}) %all-to-all-start.2) | async-done | bytes 294944 | tf_op jit(solution)/shard_map/all_to_all | solution.py:224
  110.1 0.6 slice.25
  (14 shorter events, 0.8 us)
Async XLA Ops:
  2.2 7.2 %copy-start.1 = (bf16[16,512]{1,0:T(8,128)(2,1)S(1)}, bf16[16,512]{1,0:T(8,128)(2,1)}, u32[]{:S(2)}) copy-start(bf16[16,512]{1,0:T(8,128)(2,1)} %param.6) | copy-start | bytes 49156
  2.2 7.2 %copy-start.2 = (bf16[16,64]{1,0:T(8,128)(2,1)S(1)}, bf16[16,64]{1,0:T(8,128)(2,1)}, u32[]{:S(2)}) copy-start(bf16[16,64]{1,0:T(8,128)(2,1)} %param.7) | copy-start | bytes 6148
  2.2 20.5 %all-to-all-start.1 = ((bf16[8,32,576]{2,1,0:T(8,128)(2,1)}), bf16[8,32,576]{2,1,0:T(8,128)(2,1)S(1)}, u32[]{:S(2)}, u32[]{:S(2)}) async-start(bf16[8,32,576]{2,1,0:T(8,128)(2,1)} %broadcast_in_dim.21), calls=%async_computation.1 | async-start | bytes 655360 | tf_op jit(solution)/shard_map/all_to_all | solution.py:218
  23.4 27.7 %copy-start = (bf16[1,6,128,128]{3,2,1,0:T(8,128)(2,1)S(1)}, bf16[1,6,128,128]{3,2,1,0:T(8,128)(2,1)}, u32[]{:S(2)}) copy-start(bf16[1,6,128,128]{3,2,1,0:T(8,128)(2,1)} %param.11) | copy-start | bytes 589828
  23.4 24.2 %all-to-all-start = ((bf16[16,16,576]{2,1,0:T(8,128)(2,1)}), bf16[16,16,576]{2,1,0:T(8,128)(2,1)S(1)}, u32[]{:S(2)}, u32[]{:S(2)}) async-start(bf16[16,16,576]{2,1,0:T(8,128)(2,1)} %broadcast_in_dim.20), calls=%async_computation | async-start | bytes 655360 | tf_op jit(solution)/shard_map/all_to_all | solution.py:218
  36.0 14.2 %collective-permute-start.1 = (bf16[8,32,576]{2,1,0:T(8,128)(2,1)S(1)}, bf16[8,32,576]{2,1,0:T(8,128)(2,1)S(1)}, u32[]{:S(2)}, u32[]{:S(2)}) collective-permute-start(bf16[8,32,576]{2,1,0:T(8,128)(2,1)S(1)} %all-to-all-done.1.i_own), channel_id=1, source_target_pairs={{0,32},{32,0},{1,33},{33,1},{2,34},{34,2},{3,35},{35,3},{4,36},{36... | collective-permute-start | bytes 884744 | tf_op jit(solution)/shard_map/ppermute | solution.py:233
  47.6 3.5 %collective-permute-start = (bf16[16,16,576]{2,1,0:T(8,128)(2,1)S(1)}, bf16[16,16,576]{2,1,0:T(8,128)(2,1)S(1)}, u32[]{:S(2)}, u32[]{:S(2)}) collective-permute-start(bf16[16,16,576]{2,1,0:T(8,128)(2,1)S(1)} %all-to-all-done.q_own), channel_id=1, source_target_pairs={{0,1},{1,0},{2,3},{3,2},{4,5},{5,4},{6,7},{7,6},{8,9},{9,8},{10,11... | collective-permute-start | bytes 884744 | tf_op jit(solution)/shard_map/ppermute | solution.py:235
  49.5 0.7 copy-start.3
  65.2 11.6 %collective-permute-start.3 = (bf16[8,32,576]{2,1,0:T(8,128)(2,1)S(1)}, bf16[8,32,576]{2,1,0:T(8,128)(2,1)S(1)}, u32[]{:S(2)}, u32[]{:S(2)}) collective-permute-start(bf16[8,32,576]{2,1,0:T(8,128)(2,1)S(1)} %get-tuple-element.11), channel_id=1, source_target_pairs={{0,32},{32,0},{1,33},{33,1},{2,34},{34,2},{3,35},{35,3},{4,36},{36... | collective-permute-start | bytes 884744 | tf_op jit(solution)/shard_map/ppermute | solution.py:222
  67.7 13.4 %collective-permute-start.2 = (bf16[16,16,576]{2,1,0:T(8,128)(2,1)S(1)}, bf16[16,16,576]{2,1,0:T(8,128)(2,1)S(1)}, u32[]{:S(2)}, u32[]{:S(2)}) collective-permute-start(bf16[16,16,576]{2,1,0:T(8,128)(2,1)S(1)} %get-tuple-element.9), channel_id=1, source_target_pairs={{0,1},{1,0},{2,3},{3,2},{4,5},{5,4},{6,7},{7,6},{8,9},{9,8},{10,11... | collective-permute-start | bytes 884744 | tf_op jit(solution)/shard_map/ppermute | solution.py:222
  77.6 16.3 %all-to-all-start.3 = ((bf16[8,32,576]{2,1,0:T(8,128)(2,1)}), bf16[8,32,576]{2,1,0:T(8,128)(2,1)S(1)}, u32[]{:S(2)}, u32[]{:S(2)}) async-start(bf16[8,32,576]{2,1,0:T(8,128)(2,1)} %add_convert_fusion), calls=%async_computation.3 | async-start | bytes 655360 | tf_op jit(solution)/shard_map/all_to_all | solution.py:224
  94.0 15.5 %all-to-all-start.2 = ((bf16[16,16,576]{2,1,0:T(8,128)(2,1)}), bf16[16,16,576]{2,1,0:T(8,128)(2,1)S(1)}, u32[]{:S(2)}, u32[]{:S(2)}) async-start(bf16[16,16,576]{2,1,0:T(8,128)(2,1)} %add_convert_fusion.1), calls=%async_computation.2 | async-start | bytes 655360 | tf_op jit(solution)/shard_map/all_to_all | solution.py:224

commit v5 on v4

--- a/solution.py
+++ b/solution.py
@@ -30,35 +30,57 @@
 
 def tile_kernel(
     ids, q_own, q_other, i_own, i_other, t_ref, q_keep, q_send, i_keep, i_send,
-    q_ref, i_ref, gq_ref, gi_ref,
+    q_ref, q_gate, i_gate, out, gate,
     qt, it, eqt, eit, vt, xt, tile_t, n_0, ft, fit, acc_q, acc_i, weight,
 ):
     core = ids[t_ref.shape[0]]
     side = ids[t_ref.shape[0] + 1]
 
-    def places(index, whole, half):
-        size = half.shape[1]
-        for g in range(half.shape[0]):
-            mine = pl.multiple_of(g * 2 * size + index * size, size)
-            theirs = pl.multiple_of(g * 2 * size + (1 - index) * size, size)
-            yield g, whole.at[pl.ds(mine, size), :], whole.at[pl.ds(theirs, size), :]
-
-    for g, mine, theirs in places(core, q_ref, q_own):
-        mine[...] = q_own[g]
-        theirs[...] = q_other[g]
-    for g, mine, theirs in places(side, i_ref, i_own):
-        mine[...] = i_own[g]
-        theirs[...] = i_other[g]
-
-    rows = q_ref.shape[0]
-    cols = i_ref.shape[0]
+    rows = q_ref.shape[1]
+    cols = i_gate.shape[0]
     extent = t_ref.shape[-1]
-    width = KQ * E
+    lanes = q_ref.shape[2]
+    chunks = KQ * E // lanes
     comps = KQ * KI
     blocks = cols // extent
     step = 2 * E
     chunk = KI * step
 
+    def places(index, parts, size):
+        for g in range(parts):
+            yield g, pl.multiple_of(g * 2 * size + index * size, size)
+
+    def unpack(index, parts, embeds, gates):
+        size = parts.shape[1] * lanes // (chunks * lanes + comps)
+        half = size // 2
+        for g, at in places(index, parts.shape[0], size):
+            for j in range(chunks):
+                embeds[j, pl.ds(at, size), :] = parts[g, j * size:(j + 1) * size, :].astype(
+                    embeds.dtype
+                )
+            tail = parts[g, chunks * size:, :].astype(F32)
+            gates[pl.ds(at, half), :] = tail[:, :comps]
+            gates[pl.ds(pl.multiple_of(at + half, half), half), :] = tail[:, comps:]
+
+    def pack(index, parts):
+        size = parts.shape[1] * lanes // (chunks * lanes + comps)
+        half = size // 2
+        for g, at in places(index, parts.shape[0], size):
+            for j in range(chunks):
+                parts[g, j * size:(j + 1) * size, :] = out[j, pl.ds(at, size), :].astype(
+                    parts.dtype
+                )
+            first = gate[pl.ds(at, half), :]
+            last = gate[pl.ds(pl.multiple_of(at + half, half), half), :]
+            parts[g, chunks * size:, :] = jnp.concatenate([first, last], axis=1).astype(
+                parts.dtype
+            )
+
+    unpack(core, q_own, q_ref, q_gate)
+    unpack(1 - core, q_other, q_ref, q_gate)
+    unpack(side, i_own, out, i_gate)
+    unpack(1 - side, i_other, out, i_gate)
+
     tile_t[...] = jnp.zeros_like(tile_t)
     for slot in range(t_ref.shape[0]):
         tile_id = ids[slot]
@@ -67,13 +89,14 @@
         def _():
             tile_t[tile_id] = t_ref[slot].astype(F32)
 
-    gates = q_ref[:, width:].astype(F32)
+    gates = q_gate[...]
     eq = jnp.exp(gates - jnp.max(gates, axis=1, keepdims=True))
     gates_t = gates.T
     eqt[...] = jnp.exp(gates_t - jnp.max(gates_t, axis=0, keepdims=True))
-    eit[...] = jnp.exp(i_ref[:, width:].astype(F32).T)
-    qt[...] = q_ref[:, :width].astype(F32).T
-    it[...] = i_ref[:, :width].astype(F32).T
+    eit[...] = jnp.exp(i_gate[...].T)
+    for j in range(chunks):
+        qt[j * lanes:(j + 1) * lanes, :] = q_ref[j].astype(F32).T
+        it[j * lanes:(j + 1) * lanes, :] = out[j].T
 
     eq_hi, eq_mid = split(eq)
     eq_lo = (eq - eq_hi.astype(F32) - eq_mid.astype(F32)).astype(BF)
@@ -93,7 +116,7 @@
     def spread(ap, carry):
         pick = jnp.where(part_row == lane_comp + 2 * KI * ap, 1.0, 0.0).astype(BF)
         scale = dot(parts, pick)
-        own = q_ref[:, pl.ds(pl.multiple_of(ap * step, step), step)].astype(F32)
+        own = q_ref[ap].astype(F32)
         x_rows = (scale * jnp.concatenate([own] * KI, axis=1)).astype(BF)
         for b in range(KI):
             for half in range(2):
@@ -152,24 +175,37 @@
 
     lax.fori_loop(0, KQ // 2, collect, 0)
 
-    gq_ref[:, :width] = acc_q[...].T
-    gq_ref[:, width:] = (ft[...] - eqt[...] * mean_q).T
-    for g, mine, theirs in places(core, gq_ref, q_keep):
-        q_keep[g] = mine[...]
-        q_send[g] = theirs[...].astype(BF)
-    gi_ref[:, :width] = acc_i[...].T
-    gi_ref[:, width:] = (fit[...] - eit[...] * mean_i).T
-    for g, mine, theirs in places(side, gi_ref, i_keep):
-        i_keep[g] = mine[...]
-        i_send[g] = theirs[...].astype(BF)
+    for j in range(chunks):
+        out[j] = acc_q[j * lanes:(j + 1) * lanes, :].T
+    gate[...] = (ft[...] - eqt[...] * mean_q).T
+    pack(core, q_keep)
+    pack(1 - core, q_send)
+    for j in range(chunks):
+        out[j] = acc_i[j * lanes:(j + 1) * lanes, :].T
+    gate[...] = (fit[...] - eit[...] * mean_i).T
+    pack(side, i_keep)
+    pack(1 - side, i_send)
+
+
+def total_kernel(terms, embeds, gates):
+    total = jnp.sum(terms[...].astype(F32), axis=0)
+    size, width = embeds.shape
+    lanes = total.shape[1]
+    half = size // 2
+    comps = gates.shape[1]
+    for j in range(width // lanes):
+        embeds[:, j * lanes:(j + 1) * lanes] = total[j * size:(j + 1) * size, :].astype(BF)
+    tail = total[width // lanes * size:, :]
+    gates[:half, :] = tail[:, :comps]
+    gates[half:, :] = tail[:, comps:]
 
 
 def tile_grads(scalars, cotangents, q_own, q_other, i_own, i_other, interpret=False):
-    packed = q_own.shape[-1]
-    rows = 2 * q_own.shape[0] * q_own.shape[1]
-    cols = 2 * i_own.shape[0] * i_own.shape[1]
+    lanes = q_own.shape[-1]
     width = KQ * E
     comps = KQ * KI
+    rows = 2 * q_own.shape[0] * q_own.shape[1] * lanes // (width + comps)
+    cols = 2 * i_own.shape[0] * i_own.shape[1] * lanes // (width + comps)
     extent = cotangents.shape[-1]
     vmem = pl.BlockSpec(memory_space=pltpu.VMEM)
     return pl.pallas_call(
@@ -183,10 +219,11 @@
         in_specs=[pl.BlockSpec(memory_space=pltpu.SMEM)] + [vmem] * 5,
         out_specs=(vmem,) * 4,
         scratch_shapes=[
-            pltpu.VMEM((rows, packed), BF),
-            pltpu.VMEM((cols, packed), BF),
-            pltpu.VMEM((rows, packed), F32),
-            pltpu.VMEM((cols, packed), F32),
+            pltpu.VMEM((width // lanes, rows, lanes), BF),
+            pltpu.VMEM((rows, comps), F32),
+            pltpu.VMEM((cols, comps), F32),
+            pltpu.VMEM((width // lanes, rows, lanes), F32),
+            pltpu.VMEM((rows, comps), F32),
             pltpu.VMEM((width, rows), F32),
             pltpu.VMEM((width, cols), F32),
             pltpu.VMEM((comps, rows), F32),
@@ -212,9 +249,29 @@
 ITEM = ("x_hi", "z", "core")
 
 
+def copy_kernel(embeds, gates, copies):
+    size, width = embeds.shape
+    lanes = copies.shape[2]
+    half = size // 2
+    values = gates[...].astype(F32)
+    tail = jnp.concatenate([values[:half], values[half:]], axis=1).astype(BF)
+    for g in range(copies.shape[0]):
+        for j in range(width // lanes):
+            copies[g, j * size:(j + 1) * size, :] = embeds[:, j * lanes:(j + 1) * lanes]
+        copies[g, width // lanes * size:, :] = tail
+
+
 def fetch(rows, gates, axes):
-    packed = jnp.concatenate([rows, gates], axis=1)
-    copies = jnp.broadcast_to(packed[None], (lax.axis_size(axes),) + packed.shape)
+    lanes = 2 * gates.shape[1]
+    packed = rows.shape[0] * (rows.shape[1] + gates.shape[1]) // lanes
+    vmem = pl.BlockSpec(memory_space=pltpu.VMEM)
+    copies = pl.pallas_call(
+        copy_kernel,
+        out_shape=jax.ShapeDtypeStruct((lax.axis_size(axes), packed, lanes), BF),
+        in_specs=[vmem, vmem],
+        out_specs=vmem,
+        compiler_params=pltpu.CompilerParams(vmem_limit_bytes=8 * 2**20),
+    )(rows, gates)
     return lax.all_to_all(copies, axes, 0, 0)
 
 
@@ -222,8 +279,19 @@
     got = lax.ppermute(send, pair, SWAP)
     total = (keep + got.astype(F32)).astype(BF)
     terms = lax.all_to_all(total, axes, 0, 0)
-    total = jnp.sum(terms.astype(F32), axis=0)
-    return total[:, :width].astype(BF), total[:, width:]
+    comps = KQ * KI
+    size = terms.shape[1] * terms.shape[2] // (width + comps)
+    vmem = pl.BlockSpec(memory_space=pltpu.VMEM)
+    return pl.pallas_call(
+        total_kernel,
+        out_shape=(
+            jax.ShapeDtypeStruct((size, width), BF),
+            jax.ShapeDtypeStruct((size, comps), F32),
+        ),
+        in_specs=[vmem],
+        out_specs=(vmem, vmem),
+        compiler_params=pltpu.CompilerParams(vmem_limit_bytes=8 * 2**20),
+    )(terms)
 
 
 def on_device(queries, gate_query, items, gate_items, slot_tiles, d_scores):

time: 111 us -> 108 us (0.973)
  waiting for transfers between devices: 52.3 us -> 49 us
  Pallas kernels: 14.1 us -> 17.3 us
  local copies, waits for them, and re-layouts: 4.6 us -> 2.11 us
    pallas_call x0 -> x4, Pallas kernels: none -> 2.99 us  [the longest x2 1.58 us: fetch(): pl.pallas_call(copy_kernel, out_shape=jax.ShapeDtypeStruct((lax.axis_size...]
    slice x4 -> x0, local copies, waits for them, and re-layouts: 2.44 us -> none  [give(): return (total[:, :width].astype(BF), total[:, width:])]
    all_to_all x2, waiting for transfers between devices: 22.3 us -> 20.2 us  [fetch(): return lax.all_to_all(copies, axes, 0, 0)]
    broadcast_in_dim x2 -> x0, local copies, waits for them, and re-layouts: 1.5 us -> none  [fetch(): jnp.broadcast_to(packed[None], (lax.axis_size(axes),) + packed.shape)]
    unnamed x8 -> x12, local copies, waits for them, and re-layouts: 0.66 us -> 2.11 us
  transfers between devices with their start and end apart: 8 -> 8, of which waited for: 6 -> 6; matrix products, arithmetic and copies ran while one was open for 3% -> 2% of each run, Pallas kernels for 0% -> 1%
where the time goes in v5:
time: 108 us; the launch traced here: 107 us
  waiting for transfers between devices  49 us (45%)
  starting transfers between devices  36.3 us (34%)
  Pallas kernels  17.3 us (16%)
  local copies, waits for them, and re-layouts  2.11 us (2%)
  other arithmetic  1.63 us (2%)
    all_to_all x2, waiting for transfers between devices, give(): terms = lax.all_to_all(total, axes, 0, 0)  21.5 us
    all_to_all x2, waiting for transfers between devices, fetch(): return lax.all_to_all(copies, axes, 0, 0)  20.2 us
    all_to_all x2, starting transfers between devices, fetch(): return lax.all_to_all(copies, axes, 0, 0)  19.7 us
    pallas_call x1, Pallas kernels, tile_grads(): pl.pallas_call(tile_kernel, out_shape=(jax.ShapeDtypeStruct(q_own.shape,...  14.3 us
    all_to_all x2, starting transfers between devices, give(): terms = lax.all_to_all(total, axes, 0, 0)  7.78 us
    ppermute x2, waiting for transfers between devices, give(): got = lax.ppermute(send, pair, SWAP)  6.49 us
    ppermute x2, starting transfers between devices, give(): got = lax.ppermute(send, pair, SWAP)  4.42 us
    ppermute x1, starting transfers between devices, on_device(): i_other = lax.ppermute(i_own, 'x_lo', SWAP)  2.49 us
  transfers between devices with their start and end apart: 8, of which 6 were waited for; matrix products, arithmetic and copies ran while one was open for 2% of the time, Pallas kernels for 1%

profile of v5, /device:TPU:64, one launch (start us, length us, event | category | flops | bytes accessed | tf_op | source)
XLA Modules:
  0.0 107.0 jit_solution(13963765875660686922)
XLA Ops:
  0.6 0.7 copy-done.1
  1.4 0.7 copy-done.3
  2.1 0.8 shard_map.94
  2.9 7.2 %all-to-all-start.1 = ((bf16[8,144,128]{2,1,0:T(8,128)(2,1)}), bf16[8,144,128]{2,1,0:T(8,128)(2,1)S(1)}, u32[]{:S(2)}, u32[]{:S(2)}) async-start(bf16[8,144,128]{2,1,0:T(8,128)(2,1)} %shard_map.94), calls=%async_computation.1 | async-start | bytes 589824 | tf_op jit(solution)/shard_map/all_to_all | solution.py:275
  10.1 0.8 shard_map.93
  10.9 11.8 %all-to-all-done.1.i_own = bf16[8,144,128]{2,1,0:T(8,128)(2,1)S(1)} async-done(((bf16[8,144,128]{2,1,0:T(8,128)(2,1)}), bf16[8,144,128]{2,1,0:T(8,128)(2,1)S(1)}, u32[]{:S(2)}, u32[]{:S(2)}) %all-to-all-start.1) | async-done | bytes 294944 | tf_op jit(solution)/shard_map/all_to_all | solution.py:275
  22.7 12.4 %all-to-all-start = ((bf16[16,72,128]{2,1,0:T(8,128)(2,1)}), bf16[16,72,128]{2,1,0:T(8,128)(2,1)S(1)}, u32[]{:S(2)}, u32[]{:S(2)}) async-start(bf16[16,72,128]{2,1,0:T(8,128)(2,1)} %shard_map.93), calls=%async_computation | async-start | bytes 589824 | tf_op jit(solution)/shard_map/all_to_all | solution.py:275
  35.1 2.5 %collective-permute-start.1 = (bf16[8,144,128]{2,1,0:T(8,128)(2,1)S(1)}, bf16[8,144,128]{2,1,0:T(8,128)(2,1)S(1)}, u32[]{:S(2)}, u32[]{:S(2)}) collective-permute-start(bf16[8,144,128]{2,1,0:T(8,128)(2,1)S(1)} %all-to-all-done.1.i_own), channel_id=1, source_target_pairs={{0,32},{32,0},{1,33},{33,1},{2,34},{34,2},{3,35},{35,3},{4,36},{36... | collective-permute-start | bytes 884744 | tf_op jit(solution)/shard_map/ppermute | solution.py:301
  37.6 8.4 %all-to-all-done.q_own = bf16[16,72,128]{2,1,0:T(8,128)(2,1)S(1)} async-done(((bf16[16,72,128]{2,1,0:T(8,128)(2,1)}), bf16[16,72,128]{2,1,0:T(8,128)(2,1)S(1)}, u32[]{:S(2)}, u32[]{:S(2)}) %all-to-all-start) | async-done | bytes 294944 | tf_op jit(solution)/shard_map/all_to_all | solution.py:275
  46.0 1.9 %collective-permute-start = (bf16[16,72,128]{2,1,0:T(8,128)(2,1)S(1)}, bf16[16,72,128]{2,1,0:T(8,128)(2,1)S(1)}, u32[]{:S(2)}, u32[]{:S(2)}) collective-permute-start(bf16[16,72,128]{2,1,0:T(8,128)(2,1)S(1)} %all-to-all-done.q_own), channel_id=1, source_target_pairs={{0,1},{1,0},{2,3},{3,2},{4,5},{5,4},{6,7},{7,6},{8,9},{9,8},{10,11... | collective-permute-start | bytes 884744 | tf_op jit(solution)/shard_map/ppermute | solution.py:303
  48.0 0.6 copy-done.5
  48.7 0.8 collective-permute-done.q_other
  49.5 14.3 %shard_map.95 = (f32[16,72,128]{2,1,0:T(8,128)S(1)}, bf16[16,72,128]{2,1,0:T(8,128)(2,1)S(1)}, f32[8,144,128]{2,1,0:T(8,128)S(1)}, bf16[8,144,128]{2,1,0:T(8,128)(2,1)S(1)}) custom-call(s32[8]{0:T(128)S(1)} %pad_add_fusion.ids, bf16[16,72,128]{2,1,0:T(8,128)(2,1)S(1)} %all-to-all-done.q_own, bf16[16,72,128]{2,1,0:T(8,128)(2,1)S(1)} %collective-permute-done.q_other, ...), custom_call_target="tpu_custom_call" | custom-call | tf_op jit(solution)/shard_map/pallas_call | solution.py:211
  63.8 2.5 %collective-permute-start.3 = (bf16[8,144,128]{2,1,0:T(8,128)(2,1)S(1)}, bf16[8,144,128]{2,1,0:T(8,128)(2,1)S(1)}, u32[]{:S(2)}, u32[]{:S(2)}) collective-permute-start(bf16[8,144,128]{2,1,0:T(8,128)(2,1)S(1)} %get-tuple-element.17), channel_id=1, source_target_pairs={{0,32},{32,0},{1,33},{33,1},{2,34},{34,2},{3,35},{35,3},{4,36},{36... | collective-permute-start | bytes 884744 | tf_op jit(solution)/shard_map/ppermute | solution.py:279
  66.3 1.9 %collective-permute-start.2 = (bf16[16,72,128]{2,1,0:T(8,128)(2,1)S(1)}, bf16[16,72,128]{2,1,0:T(8,128)(2,1)S(1)}, u32[]{:S(2)}, u32[]{:S(2)}) collective-permute-start(bf16[16,72,128]{2,1,0:T(8,128)(2,1)S(1)} %get-tuple-element.13), channel_id=1, source_target_pairs={{0,1},{1,0},{2,3},{3,2},{4,5},{5,4},{6,7},{7,6},{8,9},{9,8},{10,11... | collective-permute-start | bytes 884744 | tf_op jit(solution)/shard_map/ppermute | solution.py:279
  68.2 6.5 %collective-permute-done.3 = bf16[8,144,128]{2,1,0:T(8,128)(2,1)S(1)} collective-permute-done((bf16[8,144,128]{2,1,0:T(8,128)(2,1)S(1)}, bf16[8,144,128]{2,1,0:T(8,128)(2,1)S(1)}, u32[]{:S(2)}, u32[]{:S(2)}) %collective-permute-start.3) | collective-permute-done | bytes 294944 | tf_op jit(solution)/shard_map/ppermute | solution.py:279
  74.7 0.8 add_convert_fusion
  75.5 3.4 %all-to-all-start.3 = ((bf16[8,144,128]{2,1,0:T(8,128)(2,1)}), bf16[8,144,128]{2,1,0:T(8,128)(2,1)S(1)}, u32[]{:S(2)}, u32[]{:S(2)}) async-start(bf16[8,144,128]{2,1,0:T(8,128)(2,1)} %add_convert_fusion), calls=%async_computation.3 | async-start | bytes 589824 | tf_op jit(solution)/shard_map/all_to_all | solution.py:281
  78.9 0.8 add_convert_fusion.1
  79.7 11.4 %all-to-all-done.3.terms = bf16[8,144,128]{2,1,0:T(8,128)(2,1)S(1)} async-done(((bf16[8,144,128]{2,1,0:T(8,128)(2,1)}), bf16[8,144,128]{2,1,0:T(8,128)(2,1)S(1)}, u32[]{:S(2)}, u32[]{:S(2)}) %all-to-all-start.3) | async-done | bytes 294944 | tf_op jit(solution)/shard_map/all_to_all | solution.py:281
  91.1 4.4 %all-to-all-start.2 = ((bf16[16,72,128]{2,1,0:T(8,128)(2,1)}), bf16[16,72,128]{2,1,0:T(8,128)(2,1)S(1)}, u32[]{:S(2)}, u32[]{:S(2)}) async-start(bf16[16,72,128]{2,1,0:T(8,128)(2,1)} %add_convert_fusion.1), calls=%async_computation.2 | async-start | bytes 589824 | tf_op jit(solution)/shard_map/all_to_all | solution.py:281
  95.5 0.7 shard_map.97
  96.2 10.1 %all-to-all-done.2.terms = bf16[16,72,128]{2,1,0:T(8,128)(2,1)S(1)} async-done(((bf16[16,72,128]{2,1,0:T(8,128)(2,1)}), bf16[16,72,128]{2,1,0:T(8,128)(2,1)S(1)}, u32[]{:S(2)}, u32[]{:S(2)}) %all-to-all-start.2) | async-done | bytes 294944 | tf_op jit(solution)/shard_map/all_to_all | solution.py:281
  106.3 0.7 shard_map.96
  (12 shorter events, 0.1 us)
Async XLA Ops:
  0.6 0.8 copy-start.1
  1.4 0.7 copy-start.3
  2.9 7.2 %copy-start.2 = (bf16[16,512]{1,0:T(8,128)(2,1)S(1)}, bf16[16,512]{1,0:T(8,128)(2,1)}, u32[]{:S(2)}) copy-start(bf16[16,512]{1,0:T(8,128)(2,1)} %embeds.2) | copy-start | bytes 49156
  2.9 7.2 %copy-start.4 = (bf16[16,64]{1,0:T(8,128)(2,1)S(1)}, bf16[16,64]{1,0:T(8,128)(2,1)}, u32[]{:S(2)}) copy-start(bf16[16,64]{1,0:T(8,128)(2,1)} %gates.2) | copy-start | bytes 6148
  2.9 19.8 %all-to-all-start.1 = ((bf16[8,144,128]{2,1,0:T(8,128)(2,1)}), bf16[8,144,128]{2,1,0:T(8,128)(2,1)S(1)}, u32[]{:S(2)}, u32[]{:S(2)}) async-start(bf16[8,144,128]{2,1,0:T(8,128)(2,1)} %shard_map.94), calls=%async_computation.1 | async-start | bytes 589824 | tf_op jit(solution)/shard_map/all_to_all | solution.py:275
  10.9 38.6 %copy-start = (bf16[1,6,128,128]{3,2,1,0:T(8,128)(2,1)S(1)}, bf16[1,6,128,128]{3,2,1,0:T(8,128)(2,1)}, u32[]{:S(2)}) copy-start(bf16[1,6,128,128]{3,2,1,0:T(8,128)(2,1)} %param.11) | copy-start | bytes 589828
  22.7 23.4 %all-to-all-start = ((bf16[16,72,128]{2,1,0:T(8,128)(2,1)}), bf16[16,72,128]{2,1,0:T(8,128)(2,1)S(1)}, u32[]{:S(2)}, u32[]{:S(2)}) async-start(bf16[16,72,128]{2,1,0:T(8,128)(2,1)} %shard_map.93), calls=%async_computation | async-start | bytes 589824 | tf_op jit(solution)/shard_map/all_to_all | solution.py:275
  35.1 13.6 %collective-permute-start.1 = (bf16[8,144,128]{2,1,0:T(8,128)(2,1)S(1)}, bf16[8,144,128]{2,1,0:T(8,128)(2,1)S(1)}, u32[]{:S(2)}, u32[]{:S(2)}) collective-permute-start(bf16[8,144,128]{2,1,0:T(8,128)(2,1)S(1)} %all-to-all-done.1.i_own), channel_id=1, source_target_pairs={{0,32},{32,0},{1,33},{33,1},{2,34},{34,2},{3,35},{35,3},{4,36},{36... | collective-permute-start | bytes 884744 | tf_op jit(solution)/shard_map/ppermute | solution.py:301
  46.0 3.5 %collective-permute-start = (bf16[16,72,128]{2,1,0:T(8,128)(2,1)S(1)}, bf16[16,72,128]{2,1,0:T(8,128)(2,1)S(1)}, u32[]{:S(2)}, u32[]{:S(2)}) collective-permute-start(bf16[16,72,128]{2,1,0:T(8,128)(2,1)S(1)} %all-to-all-done.q_own), channel_id=1, source_target_pairs={{0,1},{1,0},{2,3},{3,2},{4,5},{5,4},{6,7},{7,6},{8,9},{9,8},{10,11... | collective-permute-start | bytes 884744 | tf_op jit(solution)/shard_map/ppermute | solution.py:303
  48.0 0.7 copy-start.5
  63.8 10.9 %collective-permute-start.3 = (bf16[8,144,128]{2,1,0:T(8,128)(2,1)S(1)}, bf16[8,144,128]{2,1,0:T(8,128)(2,1)S(1)}, u32[]{:S(2)}, u32[]{:S(2)}) collective-permute-start(bf16[8,144,128]{2,1,0:T(8,128)(2,1)S(1)} %get-tuple-element.17), channel_id=1, source_target_pairs={{0,32},{32,0},{1,33},{33,1},{2,34},{34,2},{3,35},{35,3},{4,36},{36... | collective-permute-start | bytes 884744 | tf_op jit(solution)/shard_map/ppermute | solution.py:279
  66.3 12.6 %collective-permute-start.2 = (bf16[16,72,128]{2,1,0:T(8,128)(2,1)S(1)}, bf16[16,72,128]{2,1,0:T(8,128)(2,1)S(1)}, u32[]{:S(2)}, u32[]{:S(2)}) collective-permute-start(bf16[16,72,128]{2,1,0:T(8,128)(2,1)S(1)} %get-tuple-element.13), channel_id=1, source_target_pairs={{0,1},{1,0},{2,3},{3,2},{4,5},{5,4},{6,7},{7,6},{8,9},{9,8},{10,11... | collective-permute-start | bytes 884744 | tf_op jit(solution)/shard_map/ppermute | solution.py:279
  75.5 15.6 %all-to-all-start.3 = ((bf16[8,144,128]{2,1,0:T(8,128)(2,1)}), bf16[8,144,128]{2,1,0:T(8,128)(2,1)S(1)}, u32[]{:S(2)}, u32[]{:S(2)}) async-start(bf16[8,144,128]{2,1,0:T(8,128)(2,1)} %add_convert_fusion), calls=%async_computation.3 | async-start | bytes 589824 | tf_op jit(solution)/shard_map/all_to_all | solution.py:281
  91.1 15.2 %all-to-all-start.2 = ((bf16[16,72,128]{2,1,0:T(8,128)(2,1)}), bf16[16,72,128]{2,1,0:T(8,128)(2,1)S(1)}, u32[]{:S(2)}, u32[]{:S(2)}) async-start(bf16[16,72,128]{2,1,0:T(8,128)(2,1)} %add_convert_fusion.1), calls=%async_computation.2 | async-start | bytes 589824 | tf_op jit(solution)/shard_map/all_to_all | solution.py:281
